TPU v7x, 128 devices: a whole 4x4x4 slice. The times are simulated.
128 devices in a mesh: seq: 32 (over y, x, core), head: 4 (over z).
Axes of the slice: x: 4, y: 4, z: 4, core: 2. Of those that a mesh axis runs over, the one named last changes fastest.
Arguments:
- hidden: bfloat16 [3072, 4096], P('seq'), may hold values from -6 to 6
- norm_gain: float32 [4096], replicated, may hold values from 0.5 to 1.5
- w_query: bfloat16 [4096, 4096], P(None, 'head'), may hold values from -0.09375 to 0.09375
- w_key: bfloat16 [4096, 1024], P(None, 'head'), may hold values from -0.25 to 0.25
- w_value: bfloat16 [4096, 1024], P(None, 'head'), may hold values from -0.09375 to 0.09375
- w_out: bfloat16 [4096, 4096], P('head'), may hold values from -0.09375 to 0.09375
- stored_kv: bfloat16 [32768, 2, 8, 128], P('seq', None, 'head'), may hold values from -720 to 720
- selected: int32 [3072], replicated, may hold values from 0 to 32767, as said below
- prompt_order: int32 [8], replicated, may hold values from 0 to 7, each once
- store_slot: int32 [8], replicated, may hold values from 0 to 7, each once
Outputs:
- attn_out: bfloat16 [3072, 4096], P('seq', 'head')
- new_kv: bfloat16 [3072, 2, 8, 128], P('seq', None, 'head')
Inputs may be any that keep to these rules, and one draw needn't show every extreme that they name: `selected`: each block of 1024 prompt positions holds exactly 96 distinct entries, which stand together in that block's place of the list, increasing.
All inputs are finite; a program needn't handle non-finite values.
Results may differ from a plain program's by a relative error of at most 0.02.
The roundings to bfloat16 on the way count: a program that leaves them out, or rounds other values in their place, can miss the bound.
Values may be sent and summed in bfloat16 or wider, within the bound.
A program may use at most 192 MiB of HBM per device.

v0:
```python
import jax
import jax.numpy as jnp
from jax import lax
from jax.sharding import PartitionSpec as P

HEADS = 32
KV_HEADS = 8
HEAD_DIM = 128
PASSAGE = 4096


def sent_to_all(array, axis):
    peers = lax.axis_size(axis)
    return lax.all_to_all(
        jnp.broadcast_to(array[None], (peers, *array.shape)), axis, 0, 0, tiled=True
    )


def over_copies(array, axis):
    return sent_to_all(array, axis).max(axis=0)


def in_blocks(array, dim, peers):
    shape = array.shape
    pieces = array.reshape(*shape[:dim], peers, shape[dim] // peers, *shape[dim + 1 :])
    return jnp.moveaxis(pieces, dim, 0)


def sum_at_owner(array, axis, dim):
    pieces = in_blocks(array, dim, lax.axis_size(axis))
    arrived = lax.all_to_all(pieces, axis, split_axis=0, concat_axis=0, tiled=True)
    return arrived.astype(jnp.float32).sum(axis=0)


def rope(x, pos):
    half = HEAD_DIM // 2
    freq = 500000.0 ** (-(jnp.arange(half, dtype=jnp.float32) * 2.0 / HEAD_DIM))
    angle = pos.astype(jnp.float32)[:, None] * freq[None, :]
    cosine = jnp.cos(angle)[:, None, :]
    sine = jnp.sin(angle)[:, None, :]
    first = x[..., :half]
    second = x[..., half:]
    return jnp.concatenate([first * cosine - second * sine, second * cosine + first * sine], -1)


def attend(query, query_pos, keys, values, key_pos, keep):
    scale = 1.0 / HEAD_DIM**0.5
    scores = jnp.einsum("qkgd,nkd->qkgn", query, keys, preferred_element_type=jnp.float32) * scale
    valid = (key_pos[None, :] <= query_pos[:, None]) & keep[None, :]
    valid = valid[:, None, None, :]
    scores = jnp.where(valid, scores, -1e30)
    top = jnp.max(scores, -1)
    weights = jnp.where(valid, jnp.exp(scores - top[..., None]), 0.0)
    total = jnp.sum(weights, -1)
    summed = jnp.einsum(
        "qkgn,nkd->qkgd", weights.astype(jnp.bfloat16), values, preferred_element_type=jnp.float32
    )
    return (top, total, summed)


def combine(left, right):
    top = jnp.maximum(left[0], right[0])
    left_factor = jnp.exp(left[0] - top)
    right_factor = jnp.exp(right[0] - top)
    total = left[1] * left_factor + right[1] * right_factor
    summed = left[2] * left_factor[..., None] + right[2] * right_factor[..., None]
    return (top, total, summed)


def body(
    hidden, norm_gain, w_query, w_key, w_value, w_out, stored_kv, selected, prompt_order, store_slot
):
    seq_index = lax.axis_index("seq")
    seq_count = lax.axis_size("seq")
    rows_all = selected.shape[0]
    own_rows = hidden.shape[0]
    shard_rows = stored_kv.shape[0]
    local_kv = w_key.shape[1] // HEAD_DIM
    group = HEADS // KV_HEADS
    passages = prompt_order.shape[0]
    positions = lax.dynamic_slice_in_dim(selected, seq_index * own_rows, own_rows)
    widened = hidden.astype(jnp.float32)
    normed = (
        widened * lax.rsqrt(jnp.mean(widened * widened, -1, keepdims=True) + 1e-05) * norm_gain
    ).astype(jnp.bfloat16)
    query = rope(
        jnp.dot(normed, w_query, preferred_element_type=jnp.float32).reshape(
            own_rows, local_kv * group, HEAD_DIM
        ),
        positions,
    )
    query = query.astype(jnp.bfloat16).reshape(own_rows, local_kv, group, HEAD_DIM)
    fresh_key = rope(
        jnp.dot(normed, w_key, preferred_element_type=jnp.float32).reshape(
            own_rows, local_kv, HEAD_DIM
        ),
        positions,
    )
    fresh_value = jnp.dot(normed, w_value, preferred_element_type=jnp.float32).reshape(
        own_rows, local_kv, HEAD_DIM
    )
    new_kv = jnp.stack([fresh_key, fresh_value], 1).astype(jnp.bfloat16)
    every_kv = lax.all_gather(new_kv, "seq", axis=0, tiled=True)
    always = jnp.ones((rows_all,), jnp.bool_)
    fresh_part = attend(query, positions, every_kv[:, 0], every_kv[:, 1], selected, always)
    slots = jnp.arange(passages, dtype=jnp.int32)
    picker = (prompt_order[:, None] == slots[None, :]).astype(jnp.int32)
    slot_of_prompt = jnp.sum(picker * store_slot[None, :], 1)
    prompt_of_slot = jnp.sum(
        (slot_of_prompt[:, None] == slots[None, :]).astype(jnp.int32) * slots[:, None], 0
    )
    marked = jnp.zeros((shard_rows * seq_count,), jnp.int32).at[selected].set(1)
    every_query = lax.all_gather(query, "seq", axis=0, tiled=True)
    rows = seq_index * shard_rows + jnp.arange(shard_rows, dtype=jnp.int32)
    slot = rows // PASSAGE
    offset = rows % PASSAGE
    place = jnp.sum(
        (slot[:, None] == slots[None, :]).astype(jnp.int32) * prompt_of_slot[None, :], 1
    )
    stored_pos = place * PASSAGE + offset
    stored_keep = marked[stored_pos] == 0
    keys = stored_kv[:, 0]
    values = stored_kv[:, 1]
    factor = max(1, min(seq_count, 512 // own_rows))
    while seq_count % factor != 0:
        factor = factor - 1
    per_block = own_rows * factor
    blocks = rows_all // per_block
    grouped = every_query.reshape(blocks, per_block, local_kv, group, HEAD_DIM)
    grouped_pos = selected.reshape(blocks, per_block)

    def local_block(item):
        return attend(item[0], item[1], keys, values, stored_pos, stored_keep)

    tops, totals, sums = lax.map(local_block, (grouped, grouped_pos))
    tops = tops.reshape(rows_all, local_kv, group)
    totals = totals.reshape(rows_all, local_kv, group)
    sums = sums.reshape(rows_all, local_kv, group, HEAD_DIM)
    highest = over_copies(tops.astype(jnp.bfloat16), "seq").astype(tops.dtype)
    shrink = jnp.exp(tops - highest)
    own_sums, own_totals = (
        lax.psum_scatter(
            (sums * shrink[..., None]).astype(jnp.bfloat16), "seq", scatter_dimension=0, tiled=True
        ).astype(jnp.float32),
        lax.psum_scatter(
            (totals * shrink).astype(jnp.bfloat16), "seq", scatter_dimension=0, tiled=True
        ).astype(jnp.float32),
    )
    own_top = lax.dynamic_slice_in_dim(highest, seq_index * own_rows, own_rows, 0)
    stored_part = (own_top, own_totals, own_sums)
    merged = combine(stored_part, fresh_part)
    context = (
        (merged[2] / merged[1][..., None])
        .astype(jnp.bfloat16)
        .reshape(own_rows, local_kv * group * HEAD_DIM)
    )
    partial_value = jnp.dot(context, w_out, preferred_element_type=jnp.float32)
    attn_out = sum_at_owner(partial_value.astype(jnp.bfloat16), "head", 1).astype(jnp.bfloat16)
    return (attn_out, new_kv)


def solution(mesh):
    in_specs = (
        P("seq", None),
        P(),
        P(None, "head"),
        P(None, "head"),
        P(None, "head"),
        P("head", None),
        P("seq", None, "head", None),
        P(),
        P(),
        P(),
    )
    out_specs = (P("seq", "head"), P("seq", None, "head", None))
    return jax.shard_map(body, mesh=mesh, in_specs=in_specs, out_specs=out_specs, check_vma=False)
```

profile of v0, /device:TPU:0, one launch (start us, length us, event | category | flops | bytes accessed | tf_op | source)
XLA Modules:
  0.0 399.8 jit_solution(9148418190144245169)
XLA Ops:
  8.8 5.2 %convolution_bitcast_fusion = f32[12,8,8,128]{3,1,2,0:T(8,128)S(1)} fusion(bf16[4096,1024]{1,0:T(8,128)(2,1)} %param.14, bf16[96,4096]{1,0:T(8,128)(2,1)} %param.12, f32[4096]{0:T(1024)} %param.13, f32[96]{0:T(128)S(1)} %add_rsqrt_fusion), kind=kOutput, calls=%fused_computation.43 | convolution fusion | flops 806879232 | bytes 9585024 | tf_op jit(solution)/shard_map/dot_general | solution.py:87
  20.0 11.8 %scatter_custom_fusion = s32[32768]{0:T(1024)S(1)} fusion(s32[3072]{0:T(1024)S(1)} %compare_select_fusion, s32[3072]{0:T(1024)S(1)} %broadcast.236, s32[]{:T(128)} %constant.47.clone.1), kind=kCustom, calls=%fused_computation.63 | custom fusion | bytes 131076 | tf_op jit(solution)/shard_map/scatter | solution.py:112
  31.8 6.2 %gather_fusion = s32[1024]{0:T(1024)S(1)} fusion(s32[32768]{0:T(1024)S(1)} %scatter_custom_fusion, s32[1024]{0:T(1024)S(1)} %broadcast_clamp_fusion), kind=kCustom, calls=%fused_computation | custom fusion | bytes 12288 | tf_op jit(solution)/shard_map/gather | solution.py:121
  40.1 27.0 %all-gather.3.cloned.1.call-done = bf16[3072,2,4,128]{3,0,2,1:T(8,128)(2,1)} async-done(((bf16[96,2,4,128]{3,0,2,1:T(8,128)(2,1)}), bf16[3072,2,4,128]{3,0,2,1:T(8,128)(2,1)}) %all-gather.3.cloned.1.call-update) | async-done | bytes 6291472 | tf_op jit(solution)/shard_map/all_gather | solution.py:113
  67.1 101.1 %while.14 = (s32[]{:T(128)}, f32[8,384,2,4]{1,0,3,2:T(8,128)S(1)}, f32[8,384,2,4]{1,0,3,2:T(8,128)S(1)}, f32[8,384,2,4,128]{4,1,0,3,2:T(8,128)}, s32[1024]{0:T(1...) while((s32[]{:T(128)}, f32[8,384,2,4]{1,0,3,2:T(8,128)S(1)}, ...), condition=%wide.region_8.9_spmd, body=%wide.region_5.8_spmd.sunk | while | flops 1652287488 | bytes 43281024 | solution.py:135
  71.0 4.4 %bitcast_dynamic-update-slice_fusion.2 = f32[8,384,2,4,128]{4,1,0,3,2:T(8,128)} fusion(f32[8,384,2,4,128]{4,1,0,3,2:T(8,128)} %get-tuple-element.232, s32[]{:T(128)} %get-tuple-element.229, f32[2,384,4,1024]{3,1,2,0:T(8,128)S(1)} %get-tuple-element.216, f32[384,2,4]{0,2,1:T(4,128)S(1)} %get-tuple-element.215, ...), kind=kOutput, calls=%fused_computation.12.clone.1 | convolution fusion | flops 821035008 | bytes 15479296 | tf_op jit(solution)/shard_map/while/body/eval_jaxpr/qkgn,nkd->qkgd/dot_general | solution.py:55
  75.4 4.1 %fusion.80 = f32[384,2,4]{0,2,1:T(4,128)S(1)} fusion(f32[2,384,4,1024]{3,1,2,0:T(8,128)S(1)} %get-tuple-element.216, f32[384,2,4]{0,2,1:T(4,128)S(1)} %get-tuple-element.215, pred[384,1024]{1,0:T(8,128)(4,1)S(1)} %compare_and_fusion.2), kind=kLoop, calls=%fused_computation.8.clone.1 | loop fusion | flops 15725568 | bytes 13000704 | tf_op jit(solution)/shard_map/while/body/eval_jaxpr/reduce_sum | solution.py:54
  83.7 4.4 %bitcast_dynamic-update-slice_fusion.2 = f32[8,384,2,4,128]{4,1,0,3,2:T(8,128)} fusion(f32[8,384,2,4,128]{4,1,0,3,2:T(8,128)} %get-tuple-element.232, s32[]{:T(128)} %get-tuple-element.229, f32[2,384,4,1024]{3,1,2,0:T(8,128)S(1)} %get-tuple-element.216, f32[384,2,4]{0,2,1:T(4,128)S(1)} %get-tuple-element.215, ...), kind=kOutput, calls=%fused_computation.12.clone.1 | convolution fusion | flops 821035008 | bytes 15479296 | tf_op jit(solution)/shard_map/while/body/eval_jaxpr/qkgn,nkd->qkgd/dot_general | solution.py:55
  88.1 4.1 %fusion.80 = f32[384,2,4]{0,2,1:T(4,128)S(1)} fusion(f32[2,384,4,1024]{3,1,2,0:T(8,128)S(1)} %get-tuple-element.216, f32[384,2,4]{0,2,1:T(4,128)S(1)} %get-tuple-element.215, pred[384,1024]{1,0:T(8,128)(4,1)S(1)} %compare_and_fusion.2), kind=kLoop, calls=%fused_computation.8.clone.1 | loop fusion | flops 15725568 | bytes 13000704 | tf_op jit(solution)/shard_map/while/body/eval_jaxpr/reduce_sum | solution.py:54
  92.8 3.5 bitcast_reduce_fusion.2
  96.3 4.4 %bitcast_dynamic-update-slice_fusion.2 = f32[8,384,2,4,128]{4,1,0,3,2:T(8,128)} fusion(f32[8,384,2,4,128]{4,1,0,3,2:T(8,128)} %get-tuple-element.232, s32[]{:T(128)} %get-tuple-element.229, f32[2,384,4,1024]{3,1,2,0:T(8,128)S(1)} %get-tuple-element.216, f32[384,2,4]{0,2,1:T(4,128)S(1)} %get-tuple-element.215, ...), kind=kOutput, calls=%fused_computation.12.clone.1 | convolution fusion | flops 821035008 | bytes 15479296 | tf_op jit(solution)/shard_map/while/body/eval_jaxpr/qkgn,nkd->qkgd/dot_general | solution.py:55
  100.7 4.1 %fusion.80 = f32[384,2,4]{0,2,1:T(4,128)S(1)} fusion(f32[2,384,4,1024]{3,1,2,0:T(8,128)S(1)} %get-tuple-element.216, f32[384,2,4]{0,2,1:T(4,128)S(1)} %get-tuple-element.215, pred[384,1024]{1,0:T(8,128)(4,1)S(1)} %compare_and_fusion.2), kind=kLoop, calls=%fused_computation.8.clone.1 | loop fusion | flops 15725568 | bytes 13000704 | tf_op jit(solution)/shard_map/while/body/eval_jaxpr/reduce_sum | solution.py:54
  108.9 4.4 %bitcast_dynamic-update-slice_fusion.2 = f32[8,384,2,4,128]{4,1,0,3,2:T(8,128)} fusion(f32[8,384,2,4,128]{4,1,0,3,2:T(8,128)} %get-tuple-element.232, s32[]{:T(128)} %get-tuple-element.229, f32[2,384,4,1024]{3,1,2,0:T(8,128)S(1)} %get-tuple-element.216, f32[384,2,4]{0,2,1:T(4,128)S(1)} %get-tuple-element.215, ...), kind=kOutput, calls=%fused_computation.12.clone.1 | convolution fusion | flops 821035008 | bytes 15479296 | tf_op jit(solution)/shard_map/while/body/eval_jaxpr/qkgn,nkd->qkgd/dot_general | solution.py:55
  113.3 4.1 %fusion.80 = f32[384,2,4]{0,2,1:T(4,128)S(1)} fusion(f32[2,384,4,1024]{3,1,2,0:T(8,128)S(1)} %get-tuple-element.216, f32[384,2,4]{0,2,1:T(4,128)S(1)} %get-tuple-element.215, pred[384,1024]{1,0:T(8,128)(4,1)S(1)} %compare_and_fusion.2), kind=kLoop, calls=%fused_computation.8.clone.1 | loop fusion | flops 15725568 | bytes 13000704 | tf_op jit(solution)/shard_map/while/body/eval_jaxpr/reduce_sum | solution.py:54
  121.6 4.4 %bitcast_dynamic-update-slice_fusion.2 = f32[8,384,2,4,128]{4,1,0,3,2:T(8,128)} fusion(f32[8,384,2,4,128]{4,1,0,3,2:T(8,128)} %get-tuple-element.232, s32[]{:T(128)} %get-tuple-element.229, f32[2,384,4,1024]{3,1,2,0:T(8,128)S(1)} %get-tuple-element.216, f32[384,2,4]{0,2,1:T(4,128)S(1)} %get-tuple-element.215, ...), kind=kOutput, calls=%fused_computation.12.clone.1 | convolution fusion | flops 821035008 | bytes 15479296 | tf_op jit(solution)/shard_map/while/body/eval_jaxpr/qkgn,nkd->qkgd/dot_general | solution.py:55
  126.0 4.1 %fusion.80 = f32[384,2,4]{0,2,1:T(4,128)S(1)} fusion(f32[2,384,4,1024]{3,1,2,0:T(8,128)S(1)} %get-tuple-element.216, f32[384,2,4]{0,2,1:T(4,128)S(1)} %get-tuple-element.215, pred[384,1024]{1,0:T(8,128)(4,1)S(1)} %compare_and_fusion.2), kind=kLoop, calls=%fused_computation.8.clone.1 | loop fusion | flops 15725568 | bytes 13000704 | tf_op jit(solution)/shard_map/while/body/eval_jaxpr/reduce_sum | solution.py:54
  134.2 4.4 %bitcast_dynamic-update-slice_fusion.2 = f32[8,384,2,4,128]{4,1,0,3,2:T(8,128)} fusion(f32[8,384,2,4,128]{4,1,0,3,2:T(8,128)} %get-tuple-element.232, s32[]{:T(128)} %get-tuple-element.229, f32[2,384,4,1024]{3,1,2,0:T(8,128)S(1)} %get-tuple-element.216, f32[384,2,4]{0,2,1:T(4,128)S(1)} %get-tuple-element.215, ...), kind=kOutput, calls=%fused_computation.12.clone.1 | convolution fusion | flops 821035008 | bytes 15479296 | tf_op jit(solution)/shard_map/while/body/eval_jaxpr/qkgn,nkd->qkgd/dot_general | solution.py:55
  138.6 4.1 %fusion.80 = f32[384,2,4]{0,2,1:T(4,128)S(1)} fusion(f32[2,384,4,1024]{3,1,2,0:T(8,128)S(1)} %get-tuple-element.216, f32[384,2,4]{0,2,1:T(4,128)S(1)} %get-tuple-element.215, pred[384,1024]{1,0:T(8,128)(4,1)S(1)} %compare_and_fusion.2), kind=kLoop, calls=%fused_computation.8.clone.1 | loop fusion | flops 15725568 | bytes 13000704 | tf_op jit(solution)/shard_map/while/body/eval_jaxpr/reduce_sum | solution.py:54
  146.8 4.4 %bitcast_dynamic-update-slice_fusion.2 = f32[8,384,2,4,128]{4,1,0,3,2:T(8,128)} fusion(f32[8,384,2,4,128]{4,1,0,3,2:T(8,128)} %get-tuple-element.232, s32[]{:T(128)} %get-tuple-element.229, f32[2,384,4,1024]{3,1,2,0:T(8,128)S(1)} %get-tuple-element.216, f32[384,2,4]{0,2,1:T(4,128)S(1)} %get-tuple-element.215, ...), kind=kOutput, calls=%fused_computation.12.clone.1 | convolution fusion | flops 821035008 | bytes 15479296 | tf_op jit(solution)/shard_map/while/body/eval_jaxpr/qkgn,nkd->qkgd/dot_general | solution.py:55
  151.2 4.1 %fusion.80 = f32[384,2,4]{0,2,1:T(4,128)S(1)} fusion(f32[2,384,4,1024]{3,1,2,0:T(8,128)S(1)} %get-tuple-element.216, f32[384,2,4]{0,2,1:T(4,128)S(1)} %get-tuple-element.215, pred[384,1024]{1,0:T(8,128)(4,1)S(1)} %compare_and_fusion.2), kind=kLoop, calls=%fused_computation.8.clone.1 | loop fusion | flops 15725568 | bytes 13000704 | tf_op jit(solution)/shard_map/while/body/eval_jaxpr/reduce_sum | solution.py:54
  159.4 4.4 %bitcast_dynamic-update-slice_fusion.2 = f32[8,384,2,4,128]{4,1,0,3,2:T(8,128)} fusion(f32[8,384,2,4,128]{4,1,0,3,2:T(8,128)} %get-tuple-element.232, s32[]{:T(128)} %get-tuple-element.229, f32[2,384,4,1024]{3,1,2,0:T(8,128)S(1)} %get-tuple-element.216, f32[384,2,4]{0,2,1:T(4,128)S(1)} %get-tuple-element.215, ...), kind=kOutput, calls=%fused_computation.12.clone.1 | convolution fusion | flops 821035008 | bytes 15479296 | tf_op jit(solution)/shard_map/while/body/eval_jaxpr/qkgn,nkd->qkgd/dot_general | solution.py:55
  163.9 4.1 %fusion.80 = f32[384,2,4]{0,2,1:T(4,128)S(1)} fusion(f32[2,384,4,1024]{3,1,2,0:T(8,128)S(1)} %get-tuple-element.216, f32[384,2,4]{0,2,1:T(4,128)S(1)} %get-tuple-element.215, pred[384,1024]{1,0:T(8,128)(4,1)S(1)} %compare_and_fusion.2), kind=kLoop, calls=%fused_computation.8.clone.1 | loop fusion | flops 15725568 | bytes 13000704 | tf_op jit(solution)/shard_map/while/body/eval_jaxpr/reduce_sum | solution.py:54
  170.2 4.8 %all-to-all-start = ((bf16[32,3072,2,4]{1,3,2,0:T(4,128)(2,1)}), bf16[32,3072,2,4]{1,3,2,0:T(4,128)(2,1)S(1)}, u32[]{:S(2)}, u32[]{:S(2)}) async-start(bf16[32,3072,2,4]{1,3,2,0:T(4,128)(2,1)} %broadcast_in_dim.104), calls=%async_computation | async-start | bytes 3145728 | tf_op jit(solution)/shard_map/all_to_all | solution.py:14
  175.1 23.8 %all-to-all-done = bf16[32,3072,2,4]{1,3,2,0:T(4,128)(2,1)S(1)} async-done(((bf16[32,3072,2,4]{1,3,2,0:T(4,128)(2,1)}), bf16[32,3072,2,4]{1,3,2,0:T(4,128)(2,1)S(1)}, u32[]{:S(2)}, u32[]{:S(2)}) %all-to-all-start) | async-done | bytes 1572896 | tf_op jit(solution)/shard_map/all_to_all | solution.py:14
  201.0 10.4 %fusion.19 = bf16[3072,2,4,128]{3,0,2,1:T(8,128)(2,1)} fusion(f32[8,384,2,4,128]{4,1,0,3,2:T(8,128)} %get-tuple-element.56, f32[3072,2,4]{0,2,1:T(4,128)S(1)} %get-tuple-element.131), kind=kLoop, calls=%fused_computation.25 | loop fusion | flops 6291456 | bytes 18972672 | tf_op jit(solution)/shard_map/convert_element_type | solution.py:143
  215.1 3.6 copy-done.2
  221.6 54.3 %reduce-scatter.7.cloned.1.call-done = bf16[96,8]{1,0:T(8,128)(2,1)} async-done(((bf16[3072,8]{1,0:T(8,128)(2,1)}), bf16[96,8]{1,0:T(8,128)(2,1)}) %reduce-scatter.7.cloned.1.call-update) | async-done | bytes 1552
  276.8 88.2 %reduce-scatter.5.cloned.1.call-done = bf16[96,2,4,128]{3,0,2,1:T(8,128)(2,1)} async-done(((bf16[3072,2,4,128]{3,0,2,1:T(8,128)(2,1)}), bf16[96,2,4,128]{3,0,2,1:T(8,128)(2,1)}) %reduce-scatter.5.cloned.1.call-update) | async-done | bytes 196624 | tf_op jit(solution)/shard_map/reduce_scatter | solution.py:142
  365.0 6.2 %fusion.42 = bf16[96,2,4,128]{3,0,2,1:T(8,128)(2,1)S(1)} fusion(f32[2,3072,96,4]{1,2,3,0:T(8,128)} %copy-done.2, f32[96,2,4]{0,2,1:T(4,128)S(1)} %get-tuple-element.148, pred[96,3072]{1,0:T(8,128)(4,1)S(1)} %broadcast_compare_fusion, bf16[3072,2,2,128]{3,0,2,1:T(8,128)(2,1)} %all-gather.5.cloned.1.call-done, ...), kind=kOutput, calls=%fused_computation.48 | convolution fusion | flops 616366080 | bytes 11710464 | tf_op jit(solution)/shard_map/qkgn,nkd->qkgd/dot_general | solution.py:55
  371.4 5.0 %convolution_convert_fusion = bf16[96,4096]{1,0:T(8,128)(2,1)S(1)} fusion(bf16[96,1024]{1,0:T(8,128)(2,1)S(1)} %reshape.266, bf16[1024,4096]{1,0:T(8,128)(2,1)} %param.17), kind=kOutput, calls=%fused_computation.33 | convolution fusion | flops 805699584 | bytes 9371648 | tf_op jit(solution)/shard_map/dot_general | solution.py:157
  377.4 4.4 %all-to-all-start.1 = ((bf16[4,96,1024]{2,1,0:T(8,128)(2,1)}), bf16[4,96,1024]{2,1,0:T(8,128)(2,1)S(1)}, u32[]{:S(2)}, u32[]{:S(2)}) async-start(bf16[4,96,1024]{2,1,0:T(8,128)(2,1)} %bitcast.159), calls=%async_computation.2 | async-start | bytes 1572864 | tf_op jit(solution)/shard_map/all_to_all | solution.py:31
  382.5 9.9 %all-to-all-done.1 = bf16[4,96,1024]{2,1,0:T(8,128)(2,1)S(1)} async-done(((bf16[4,96,1024]{2,1,0:T(8,128)(2,1)}), bf16[4,96,1024]{2,1,0:T(8,128)(2,1)S(1)}, u32[]{:S(2)}, u32[]{:S(2)}) %all-to-all-start.1) | async-done | bytes 786464 | tf_op jit(solution)/shard_map/all_to_all | solution.py:31
  (137 shorter events, 52.5 us)
Async XLA Ops:
  7.2 8.5 %copy-start = (bf16[4096,256]{1,0:T(8,128)(2,1)S(1)}, bf16[4096,256]{1,0:T(8,128)(2,1)}, u32[]{:S(2)}) copy-start(bf16[4096,256]{1,0:T(8,128)(2,1)} %param.15) | copy-start | bytes 6291460
  7.2 59.9 %all-gather.3.cloned.1.call-start = ((), (), s32[]{:S(2)}) async-start(), calls=%async_computation.4 | async-start | bytes 6488064 | tf_op jit(solution)/shard_map/all_gather | solution.py:113
  8.8 5.4 %copy-start.6 = (s32[3072]{0:T(1024)S(1)}, s32[3072]{0:T(1024)}, u32[]{:S(2)}) copy-start(s32[3072]{0:T(1024)} %param.19) | copy-start | bytes 36868
  8.8 6.9 %copy-start.3 = (bf16[96,4096]{1,0:T(8,128)(2,1)S(1)}, bf16[96,4096]{1,0:T(8,128)(2,1)}, u32[]{:S(2)}) copy-start(bf16[96,4096]{1,0:T(8,128)(2,1)} %param.12) | copy-start | bytes 2359300
  8.8 6.9 %copy-start.7 = (f32[4096]{0:T(1024)S(1)}, f32[4096]{0:T(1024)}, u32[]{:S(2)}) copy-start(f32[4096]{0:T(1024)} %param.13) | copy-start | bytes 49156
  14.1 5.5 %copy-start.8 = (s32[8]{0:T(128)S(1)}, s32[8]{0:T(128)}, u32[]{:S(2)}) copy-start(s32[8]{0:T(128)} %param.21) | copy-start | bytes 100
  14.1 5.5 %copy-start.9 = (s32[8]{0:T(128)S(1)}, s32[8]{0:T(128)}, u32[]{:S(2)}) copy-start(s32[8]{0:T(128)} %param.20) | copy-start | bytes 100
  15.6 196.1 %all-gather.5.cloned.1.call-start = ((), (), s32[]{:S(2)}) async-start(), calls=%async_computation.6 | async-start | bytes 3244032 | tf_op jit(solution)/shard_map/all_gather | solution.py:103
  170.2 28.8 %all-to-all-start = ((bf16[32,3072,2,4]{1,3,2,0:T(4,128)(2,1)}), bf16[32,3072,2,4]{1,3,2,0:T(4,128)(2,1)S(1)}, u32[]{:S(2)}, u32[]{:S(2)}) async-start(bf16[32,3072,2,4]{1,3,2,0:T(4,128)(2,1)} %broadcast_in_dim.104), calls=%async_computation | async-start | bytes 3145728 | tf_op jit(solution)/shard_map/all_to_all | solution.py:14
  175.0 100.8 %reduce-scatter.7.cloned.1.call-start = ((), (), s32[]{:S(2)}) async-start(), calls=%async_computation.7 | async-start | bytes 811008
  201.0 164.0 %reduce-scatter.5.cloned.1.call-start = ((), (), s32[]{:S(2)}) async-start(), calls=%async_computation.5 | async-start | bytes 6488064 | tf_op jit(solution)/shard_map/reduce_scatter | solution.py:142
  201.0 10.7 %copy-start.5 = (bf16[96,2,4,128]{3,0,2,1:T(8,128)(2,1)S(1)}, bf16[96,2,4,128]{3,0,2,1:T(8,128)(2,1)}, u32[]{:S(2)}) copy-start(bf16[96,2,4,128]{3,0,2,1:T(8,128)(2,1)} %pad_maximum_fusion) | copy-start | bytes 589828
  215.1 3.6 copy-start.2
  371.3 21.9 %copy-start.1 = (bf16[4096,256]{1,0:T(8,128)(2,1)S(1)}, bf16[4096,256]{1,0:T(8,128)(2,1)}, u32[]{:S(2)}) copy-start(bf16[4096,256]{1,0:T(8,128)(2,1)} %param.15) | copy-start | bytes 6291460
  371.4 10.4 %copy-start.4 = (bf16[96,2,2,128]{3,0,2,1:T(8,128)(2,1)S(1)}, bf16[96,2,2,128]{3,0,2,1:T(8,128)(2,1)}, u32[]{:S(2)}) copy-start(bf16[96,2,2,128]{3,0,2,1:T(8,128)(2,1)} %pad_maximum_fusion.1) | copy-start | bytes 294916
  377.4 15.0 %all-to-all-start.1 = ((bf16[4,96,1024]{2,1,0:T(8,128)(2,1)}), bf16[4,96,1024]{2,1,0:T(8,128)(2,1)S(1)}, u32[]{:S(2)}, u32[]{:S(2)}) async-start(bf16[4,96,1024]{2,1,0:T(8,128)(2,1)} %bitcast.159), calls=%async_computation.2 | async-start | bytes 1572864 | tf_op jit(solution)/shard_map/all_to_all | solution.py:31
Sparse Core Ops, SparseCore 0:
  15.8 51.3 all-gather.2
  70.0 43.5 all-gather.4
  201.1 74.7 reduce-scatter.6
  279.5 85.4 reduce-scatter.4
where the time goes:
time: 401 us; the launch traced here: 400 us
  waiting for transfers between devices  203 us (51%)
  matrix products  85.9 us (21%)
  other arithmetic  54.7 us (14%)
  local copies, waits for them, and re-layouts  31.7 us (8%)
  between operations  14.2 us (4%)
  starting transfers between devices  9.43 us (2%)
    reduce_scatter x1, waiting for transfers between devices, body(): lax.psum_scatter((sums * shrink[..., None]).astype(jnp.bfloat16), 'seq',...  88.2 us
    unnamed x5, waiting for transfers between devices  54.4 us
    dot_general x9, matrix products, attend(): jnp.einsum('qkgn,nkd->qkgd', weights.astype(jnp.bfloat16), values, prefer...  41.4 us
    reduce_sum x9, other arithmetic, attend(): total = jnp.sum(weights, -1)  35.7 us
    dot_general x9, matrix products, attend(): jnp.einsum('qkgd,nkd->qkgn', query, keys, preferred_element_type=jnp.floa...  31.6 us
    all_gather x1, waiting for transfers between devices, body(): every_query = lax.all_gather(query, 'seq', axis=0, tiled=True)  27 us
    all_to_all x1, waiting for transfers between devices, sent_to_all(): lax.all_to_all(jnp.broadcast_to(array[None], (peers, *array.shape)), axis...  23.8 us
    scatter x1, local copies, waits for them, and re-layouts, body(): marked = jnp.zeros((shard_rows * seq_count,), jnp.int32).at[selected].set(1)  11.8 us
  transfers between devices with their start and end apart: 6, of which 5 were waited for; matrix products, arithmetic and copies ran while one was open for 37% of the time, Pallas kernels for 0%

commit v1 on v0

v1 whole, which is shorter than its diff:
```python
import functools

import jax
import jax.numpy as jnp
from jax import lax
from jax.experimental import pallas as pl
from jax.experimental.pallas import tpu as pltpu
from jax.sharding import PartitionSpec as P

HEADS = 32
KV_HEADS = 8
HEAD_DIM = 128
PASSAGE = 4096
SIDE = 4
GROUP = HEADS // KV_HEADS
BLOCK = 1024
SEL = 96
FRESH = 128
HALF_KEYS = BLOCK + FRESH
KEYS = 2 * HALF_KEYS
ROWS = GROUP * SEL
FAR = 1.0e9
NEG = -1.0e30
LOG_SCALE = 1.4426950408889634 / HEAD_DIM**0.5
F32 = jnp.float32
BF16 = jnp.bfloat16
MESH = pl.DeviceIdType.MESH


def walk(i):
    return i + i // 2 - 2 * (i // 3)


def pack_rows(column):
    lane = lax.broadcasted_iota(jnp.int32, (SEL, 128), 1)
    total = jnp.zeros((SEL, 128), F32)
    for h in range(GROUP):
        total = jnp.where(lane == h, column[h * SEL : (h + 1) * SEL], total)
    square = jnp.concatenate([total, jnp.zeros((128 - SEL, 128), F32)], 0)
    return square.T[:8]


def unpack_rows(packed):
    square = jnp.concatenate([packed, jnp.zeros((120, 128), F32)], 0).T
    return jnp.concatenate(
        [jnp.broadcast_to(square[:SEL, h : h + 1], (SEL, 128)) for h in range(GROUP)], 0
    )


def merge(parts, stats):
    top = functools.reduce(jnp.maximum, stats)
    factors = [jnp.exp2(s - top) for s in stats]
    total = functools.reduce(jnp.add, factors)
    merged = sum(
        part.astype(F32) * unpack_rows(factor / total) for part, factor in zip(parts, factors)
    )
    return merged, top + jnp.log2(total)


def kernel(
    query_in,
    key_in,
    value_in,
    key_pos,
    row_pos,
    w_out_in,
    out_ref,
    qbuf,
    kbuf,
    vbuf,
    wbuf,
    scores,
    tops,
    part,
    stat,
    rb_part,
    rb_stat,
    mid,
    mid_stat,
    ra_part,
    ra_stat,
    ctx,
    zsend,
    zrecv,
    local_sem,
    kv_ssem,
    kv_rsem,
    g_ssem,
    g_rsem,
    bp_ssem,
    bp_rsem,
    bs_ssem,
    bs_rsem,
    ap_ssem,
    ap_rsem,
    as_ssem,
    as_rsem,
    z_ssem,
    z_rsem,
):
    seq = lax.axis_index("seq")
    head = lax.axis_index("head")
    core = lax.rem(seq, 2)
    chip_x = lax.rem(seq // 2, SIDE)
    chip_y = seq // (2 * SIDE)

    def chip_seq(dx, dy):
        return (lax.rem(chip_y + dy, SIDE) * SIDE + lax.rem(chip_x + dx, SIDE)) * 2 + core

    def peer(g, da, db):
        return chip_seq(da, db) if g == 0 else chip_seq(db, da)

    def at(index):
        return (index, head)

    partner = (seq + 1 - 2 * core, head)

    barrier = pltpu.get_barrier_semaphore()
    others = [partner]
    for d in range(1, SIDE):
        others.append(at(chip_seq(d, 0)))
        others.append(at(chip_seq(0, d)))
        others.append((seq, lax.rem(head + d, SIDE)))
    for other in others:
        pl.semaphore_signal(barrier, inc=1, device_id=other, device_id_type=MESH)

    own_q = pltpu.make_async_copy(query_in, qbuf.at[:, 0], local_sem.at[0])
    own_k = pltpu.make_async_copy(key_in, kbuf.at[:, pl.ds(0, HALF_KEYS)], local_sem.at[1])
    own_v = pltpu.make_async_copy(value_in, vbuf.at[:, pl.ds(0, HALF_KEYS)], local_sem.at[2])
    own_q.start()
    own_k.start()
    own_v.start()
    weights = [
        pltpu.make_async_copy(
            w_out_in.at[:, pl.ds(n * 1024, 1024)], wbuf.at[n], local_sem.at[3 + n]
        )
        for n in range(SIDE)
    ]
    for copy in weights:
        copy.start()
    pl.semaphore_wait(barrier, len(others))

    kv_copies = [
        pltpu.make_async_remote_copy(
            src_ref=src,
            dst_ref=dst.at[:, pl.ds(HALF_KEYS, HALF_KEYS)],
            send_sem=kv_ssem.at[n],
            recv_sem=kv_rsem.at[n],
            device_id=partner,
            device_id_type=MESH,
        )
        for n, (src, dst) in enumerate(((key_in, kbuf), (value_in, vbuf)))
    ]
    for copy in kv_copies:
        copy.start()
    own_q.wait()

    def whole(g, src, dst, sem, to):
        return pltpu.make_async_remote_copy(
            src_ref=qbuf.at[g, src],
            dst_ref=qbuf.at[g, dst],
            send_sem=g_ssem.at[g, sem],
            recv_sem=g_rsem.at[g, dst, 0],
            device_id=at(to),
            device_id_type=MESH,
        )

    def halved(g, src, dst, half, sem, to):
        rows = pl.ds(half * (ROWS // 2), ROWS // 2)
        return pltpu.make_async_remote_copy(
            src_ref=qbuf.at[g, src, rows],
            dst_ref=qbuf.at[g, dst, rows],
            send_sem=g_ssem.at[g, sem],
            recv_sem=g_rsem.at[g, dst, half],
            device_id=at(to),
            device_id_type=MESH,
        )

    def a_sends(g):
        return [whole(g, 0, 12, 0, peer(g, 1, 0)), whole(g, 0, 4, 1, peer(g, 3, 0))]

    def a_forward(g, da):
        if da == 3:
            return halved(g, 12, 8, 0, 2, peer(g, 1, 0))
        return halved(g, 4, 8, 1, 3, peer(g, 3, 0))

    def b_sends(g, da):
        return [
            whole(g, da * 4, da * 4 + 3, 4 + 4 * da, peer(g, 0, 1)),
            whole(g, da * 4, da * 4 + 1, 5 + 4 * da, peer(g, 0, 3)),
        ]

    def b_forwards(g, da):
        return [
            halved(g, da * 4 + 3, da * 4 + 2, 0, 6 + 4 * da, peer(g, 0, 1)),
            halved(g, da * 4 + 1, da * 4 + 2, 1, 7 + 4 * da, peer(g, 0, 3)),
        ]

    def arrive(t, g):
        da = walk(lax.rem(t, 4))
        row = t // 4

        @pl.when(t == 0)
        def _():
            for copy in a_sends(g):
                copy.start()

        @pl.when(jnp.logical_or(t == 1, t == 2))
        def _():
            whole(g, 0, da * 4, 0, peer(g, 1, 0)).wait_recv()

        @pl.when(t == 1)
        def _():
            a_forward(g, 1).start()

        @pl.when(t == 2)
        def _():
            a_forward(g, 3).start()

        @pl.when(t == 3)
        def _():
            for half in range(2):
                halved(g, 0, 8, half, 0, peer(g, 1, 0)).wait_recv()

        @pl.when(row == 0)
        def _():
            for copy in b_sends(g, da):
                copy.start()

        @pl.when(row == 1)
        def _():
            for db in (1, 3):
                whole(g, 0, da * 4 + db, 0, peer(g, 1, 0)).wait_recv()
            for copy in b_forwards(g, da):
                copy.start()

        @pl.when(row == 2)
        def _():
            for half in range(2):
                halved(g, 0, da * 4 + 2, half, 0, peer(g, 1, 0)).wait_recv()

    def slot_of(t):
        return walk(lax.rem(t, 4)) * 4 + t // 4

    def score(t, g):
        da = walk(lax.rem(t, 4))
        owner = peer(g, da, t // 4)
        s = lax.dot_general(
            qbuf[g, slot_of(t)],
            kbuf[g],
            (((1,), (1,)), ((), ())),
            preferred_element_type=F32,
        )
        row = jnp.broadcast_to(row_pos[pl.ds(owner, 1), :], (128, 128)).T[:SEL, :1]
        pos = jnp.concatenate([row] * GROUP, 0)
        s = jnp.where(key_pos[...] <= pos, s, NEG)
        scores[g] = s
        tops[g] = jnp.broadcast_to(jnp.max(s, -1, keepdims=True), (ROWS, 128))

    def weigh(t, g):
        top = tops[g]
        e = jnp.exp2((scores[g] - top[:, :1]) * LOG_SCALE).astype(BF16)
        table = jnp.concatenate([vbuf[g], jnp.ones((KEYS, 128), BF16)], 1)
        summed = jnp.dot(e, table, preferred_element_type=F32)
        total = summed[:, 128:]
        part[g, t] = (summed[:, :128] / total).astype(BF16)
        stat[g, t] = pack_rows(top * LOG_SCALE + jnp.log2(total))

    def b_result(g, t, da, db):
        to = at(peer(g, 0, db))
        return [
            pltpu.make_async_remote_copy(
                src_ref=part.at[g, t],
                dst_ref=rb_part.at[g, da, db - 1],
                send_sem=bp_ssem.at[g, da, db - 1],
                recv_sem=bp_rsem.at[g, da, db - 1],
                device_id=to,
                device_id_type=MESH,
            ),
            pltpu.make_async_remote_copy(
                src_ref=stat.at[g, t],
                dst_ref=rb_stat.at[g, da, db - 1],
                send_sem=bs_ssem.at[g, da, db - 1],
                recv_sem=bs_rsem.at[g, da, db - 1],
                device_id=to,
                device_id_type=MESH,
            ),
        ]

    def pass_on(t, g):
        @pl.when(t >= 4)
        def _():
            for copy in b_result(g, t, walk(lax.rem(t, 4)), t // 4):
                copy.start()

    arrive(0, 0)
    arrive(0, 1)
    own_k.wait()
    own_v.wait()
    for copy in kv_copies:
        copy.wait()
    score(0, 0)

    def step(t, carry):
        @pl.when(t > 0)
        def _():
            arrive(t, 1)

        score(t, 1)
        weigh(t, 0)
        pass_on(t, 0)
        after = jnp.minimum(t + 1, 15)

        @pl.when(t < 15)
        def _():
            arrive(after, 0)

        score(after, 0)
        weigh(t, 1)
        pass_on(t, 1)
        return carry

    lax.fori_loop(0, 16, step, 0)

    def a_result(g, da):
        to = at(peer(g, da, 0))
        return [
            pltpu.make_async_remote_copy(
                src_ref=mid.at[g, da - 1],
                dst_ref=ra_part.at[g, da - 1],
                send_sem=ap_ssem.at[g, da - 1],
                recv_sem=ap_rsem.at[g, da - 1],
                device_id=to,
                device_id_type=MESH,
            ),
            pltpu.make_async_remote_copy(
                src_ref=mid_stat.at[g, da - 1],
                dst_ref=ra_stat.at[g, da - 1],
                send_sem=as_ssem.at[g, da - 1],
                recv_sem=as_rsem.at[g, da - 1],
                device_id=to,
                device_id_type=MESH,
            ),
        ]

    def line_sum(g, da, t):
        for db in range(1, SIDE):
            for copy in b_result(g, 0, da, db):
                copy.wait_recv()
        return merge(
            [part[g, t]] + [rb_part[g, da, n] for n in range(3)],
            [stat[g, t]] + [rb_stat[g, da, n] for n in range(3)],
        )

    for da, t in ((2, 3), (1, 1), (3, 2)):
        for g in range(2):
            merged, logs = line_sum(g, da, t)
            mid[g, da - 1] = merged.astype(BF16)
            mid_stat[g, da - 1] = logs
            for copy in a_result(g, da):
                copy.start()
    for g in range(2):
        merged, logs = line_sum(g, 0, 0)
        part[g, 0] = merged.astype(BF16)
        stat[g, 0] = logs
    for g in range(2):
        for da in (1, 3, 2):
            for copy in a_result(g, da):
                copy.wait_recv()
        merged, _ = merge(
            [part[g, 0]] + [ra_part[g, n] for n in range(3)],
            [stat[g, 0]] + [ra_stat[g, n] for n in range(3)],
        )
        for h in range(GROUP):
            ctx[:, pl.ds((g * GROUP + h) * 128, 128)] = merged[h * SEL : (h + 1) * SEL].astype(BF16)

    for copy in weights:
        copy.wait()

    def z_result(dz):
        return pltpu.make_async_remote_copy(
            src_ref=zsend.at[dz - 1],
            dst_ref=zrecv.at[dz - 1],
            send_sem=z_ssem.at[dz - 1],
            recv_sem=z_rsem.at[dz - 1],
            device_id=(seq, lax.rem(head + dz, SIDE)),
            device_id_type=MESH,
        )

    for dz in (2, 1, 3):
        zsend[dz - 1] = jnp.dot(
            ctx[...], wbuf[lax.rem(head + dz, SIDE)], preferred_element_type=F32
        ).astype(BF16)
        z_result(dz).start()
    total = jnp.dot(ctx[...], wbuf[head], preferred_element_type=F32).astype(BF16).astype(F32)
    for dz in (1, 3, 2):
        z_result(dz).wait_recv()
        total = total + zrecv[dz - 1].astype(F32)
    out_ref[...] = total.astype(BF16)

    for g in range(2):
        for copy in a_sends(g) + [a_forward(g, 3), a_forward(g, 1)]:
            copy.wait_send()
        for da in range(4):
            for copy in b_sends(g, da) + b_forwards(g, da):
                copy.wait_send()
            for db in range(1, 4):
                for copy in b_result(g, 0, da, db):
                    copy.wait_send()
        for da in range(1, 4):
            for copy in a_result(g, da):
                copy.wait_send()
    for dz in range(1, 4):
        z_result(dz).wait_send()


def attend(query, keys, values, key_pos, row_pos, w_out):
    vmem = pl.BlockSpec(memory_space=pltpu.VMEM)
    hbm = pl.BlockSpec(memory_space=pl.ANY)
    dma = pltpu.SemaphoreType.DMA
    return pl.pallas_call(
        kernel,
        out_shape=jax.ShapeDtypeStruct((SEL, 1024), BF16),
        in_specs=[hbm, hbm, hbm, vmem, vmem, hbm],
        out_specs=vmem,
        scratch_shapes=[
            pltpu.VMEM((2, 16, ROWS, 128), BF16),
            pltpu.VMEM((2, KEYS, 128), BF16),
            pltpu.VMEM((2, KEYS, 128), BF16),
            pltpu.VMEM((SIDE, 1024, 1024), BF16),
            pltpu.VMEM((2, ROWS, KEYS), F32),
            pltpu.VMEM((2, ROWS, 128), F32),
            pltpu.VMEM((2, 16, ROWS, 128), BF16),
            pltpu.VMEM((2, 16, 8, 128), F32),
            pltpu.VMEM((2, 4, 3, ROWS, 128), BF16),
            pltpu.VMEM((2, 4, 3, 8, 128), F32),
            pltpu.VMEM((2, 3, ROWS, 128), BF16),
            pltpu.VMEM((2, 3, 8, 128), F32),
            pltpu.VMEM((2, 3, ROWS, 128), BF16),
            pltpu.VMEM((2, 3, 8, 128), F32),
            pltpu.VMEM((SEL, 1024), BF16),
            pltpu.VMEM((3, SEL, 1024), BF16),
            pltpu.VMEM((3, SEL, 1024), BF16),
            dma((7,)),
            dma((2,)),
            dma((2,)),
            dma((2, 20)),
            dma((2, 16, 2)),
            dma((2, 4, 3)),
            dma((2, 4, 3)),
            dma((2, 4, 3)),
            dma((2, 4, 3)),
            dma((2, 3)),
            dma((2, 3)),
            dma((2, 3)),
            dma((2, 3)),
            dma((3,)),
            dma((3,)),
        ],
        compiler_params=pltpu.CompilerParams(
            collective_id=0, has_side_effects=True, vmem_limit_bytes=60_000_000
        ),
    )(query, keys, values, key_pos, row_pos, w_out)


def rope(x, pos):
    half = HEAD_DIM // 2
    freq = 500000.0 ** (-(jnp.arange(half, dtype=jnp.float32) * 2.0 / HEAD_DIM))
    angle = pos.astype(jnp.float32)[:, None] * freq[None, :]
    cosine = jnp.cos(angle)[:, None, :]
    sine = jnp.sin(angle)[:, None, :]
    first = x[..., :half]
    second = x[..., half:]
    return jnp.concatenate([first * cosine - second * sine, second * cosine + first * sine], -1)


def body(
    hidden, norm_gain, w_query, w_key, w_value, w_out, stored_kv, selected, prompt_order, store_slot
):
    seq_index = lax.axis_index("seq")
    own_rows = hidden.shape[0]
    shard_rows = stored_kv.shape[0]
    local_kv = w_key.shape[1] // HEAD_DIM
    passages = prompt_order.shape[0]
    per_passage = PASSAGE // shard_rows
    positions = lax.dynamic_slice_in_dim(selected, seq_index * own_rows, own_rows)
    widened = hidden.astype(jnp.float32)
    normed = (
        widened * lax.rsqrt(jnp.mean(widened * widened, -1, keepdims=True) + 1e-05) * norm_gain
    ).astype(jnp.bfloat16)
    query = rope(
        jnp.dot(normed, w_query, preferred_element_type=jnp.float32).reshape(
            own_rows, local_kv * GROUP, HEAD_DIM
        ),
        positions,
    )
    query = query.astype(jnp.bfloat16).transpose(1, 0, 2).reshape(local_kv, ROWS, HEAD_DIM)
    fresh_key = rope(
        jnp.dot(normed, w_key, preferred_element_type=jnp.float32).reshape(
            own_rows, local_kv, HEAD_DIM
        ),
        positions,
    )
    fresh_value = jnp.dot(normed, w_value, preferred_element_type=jnp.float32).reshape(
        own_rows, local_kv, HEAD_DIM
    )
    new_kv = jnp.stack([fresh_key, fresh_value], 1).astype(jnp.bfloat16)

    slots = jnp.arange(passages, dtype=jnp.int32)
    picker = (prompt_order[:, None] == slots[None, :]).astype(jnp.int32)
    slot_of_prompt = jnp.sum(picker * store_slot[None, :], 1)
    prompt_of_slot = jnp.sum(
        (slot_of_prompt[:, None] == slots[None, :]).astype(jnp.int32) * slots[:, None], 0
    )

    def positions_of(device):
        place = jnp.sum(jnp.where(slots == device // per_passage, prompt_of_slot, 0))
        block = place * per_passage + device % per_passage
        there = block * shard_rows + jnp.arange(shard_rows, dtype=jnp.int32)
        replaced = lax.dynamic_slice_in_dim(selected, block * own_rows, own_rows)
        gone = jnp.any(there[:, None] == replaced[None, :], 1)
        fresh = lax.dynamic_slice_in_dim(selected, device * own_rows, own_rows)
        return [
            jnp.where(gone, FAR, there.astype(F32)),
            fresh.astype(F32),
            jnp.full((FRESH - own_rows,), FAR, F32),
        ]

    other_core = seq_index + 1 - 2 * (seq_index % 2)
    key_pos = jnp.concatenate(positions_of(seq_index) + positions_of(other_core))[None]
    row_pos = jnp.pad(
        selected.astype(F32).reshape(-1, own_rows), ((0, 0), (0, 128 - own_rows))
    )
    both = jnp.concatenate(
        [
            stored_kv,
            new_kv,
            jnp.zeros((FRESH - own_rows, *new_kv.shape[1:]), BF16),
        ],
        0,
    ).transpose(1, 2, 0, 3)
    attn_out = attend(query, both[0], both[1], key_pos, row_pos, w_out)
    return (attn_out, new_kv)


def solution(mesh):
    in_specs = (
        P("seq", None),
        P(),
        P(None, "head"),
        P(None, "head"),
        P(None, "head"),
        P("head", None),
        P("seq", None, "head", None),
        P(),
        P(),
        P(),
    )
    out_specs = (P("seq", "head"), P("seq", None, "head", None))
    return jax.shard_map(body, mesh=mesh, in_specs=in_specs, out_specs=out_specs, check_vma=False)
```

time: 401 us -> 101 us (0.25)
  waiting for transfers between devices: 203 us -> 0 us
  matrix products: 85.9 us -> 8.78 us
  Pallas kernels: 0 us -> 76.9 us
  other arithmetic: 54.7 us -> 5.84 us
  local copies, waits for them, and re-layouts: 31.7 us -> 6.77 us
  between operations: 14.2 us -> 2.23 us
  starting transfers between devices: 9.43 us -> 0 us
    reduce_scatter x1 -> x0, waiting for transfers between devices: 88.2 us -> none  [body(): lax.psum_scatter((sums * shrink[..., None]).astype(jnp.bfloat16), 'seq',...]
    dot_general x19 -> x0, matrix products: 78 us -> none  [the longest x9 41.4 us: attend(): jnp.einsum('qkgn,nkd->qkgd', weights.astype(jnp.bfloat16), values, prefer...]
    pallas_call x0 -> x1, Pallas kernels: none -> 76.9 us  [attend(): pl.pallas_call(kernel, out_shape=jax.ShapeDtypeStruct((SEL, 1024), BF16),...]
    unnamed x5 -> x0, waiting for transfers between devices: 54.4 us -> none
    reduce_sum x11 -> x1, other arithmetic: 36.6 us -> 0.64 us  [positions_of(): jnp.sum(jnp.where(slots == device // per_passage, prompt_of_slot, 0))]
    all_to_all x2 -> x0, waiting for transfers between devices: 33.7 us -> none  [the longest x1 23.8 us: sent_to_all(): lax.all_to_all(jnp.broadcast_to(array[None], (peers, *array.shape)), axis...]
    all_gather x2 -> x0, waiting for transfers between devices: 27.1 us -> none  [the longest x1 27 us: body(): every_query = lax.all_gather(query, 'seq', axis=0, tiled=True)]
    scatter x1 -> x0, local copies, waits for them, and re-layouts: 11.8 us -> none  [body(): marked = jnp.zeros((shard_rows * seq_count,), jnp.int32).at[selected].set(1)]
  transfers between devices with their start and end apart: 6 -> 0, of which waited for: 5 -> 0; matrix products, arithmetic and copies ran while one was open for 37% -> 0% of each run, Pallas kernels for 0% -> 0%
where the time goes in v1:
time: 101 us
  Pallas kernels  76.9 us (76%)
  matrix products  8.78 us (9%)
  local copies, waits for them, and re-layouts  6.77 us (7%)
  other arithmetic  5.84 us (6%)
  between operations  2.23 us (2%)
    pallas_call x1, Pallas kernels, attend(): pl.pallas_call(kernel, out_shape=jax.ShapeDtypeStruct((SEL, 1024), BF16),...  76.9 us
    dot_general x1, matrix products, body(): jnp.dot(normed, w_query, preferred_element_type=jnp.float32)  4.94 us
    unnamed x12, local copies, waits for them, and re-layouts  3.8 us
    dot_general x1, matrix products, body(): jnp.dot(normed, w_value, preferred_element_type=jnp.float32)  2.12 us

profile of v1, /device:TPU:0, one launch (start us, length us, event | category | flops | bytes accessed | tf_op | source)
XLA Modules:
  0.0 100.5 jit_solution(17941275348670608630)
XLA Ops:
  0.6 0.0 copy-start
  0.7 1.0 select_reduce_fusion.1
  1.7 0.1 select_reduce_fusion
  1.8 0.6 fusion.4
  3.8 0.9 dynamic-slice_convert_fusion
  4.6 0.2 compare_reduce_fusion
  4.9 0.1 concatenate.17
  4.9 0.6 broadcast_in_dim.15.key_pos
  5.6 0.3 multiply_cosine_fusion
  5.8 1.4 %fusion = f32[96]{0:T(128)S(1)} fusion(bf16[96,4096]{1,0:T(8,128)(2,1)} %param.10), kind=kLoop, calls=%fused_computation.2 | loop fusion | flops 1179552 | bytes 786816 | tf_op jit(solution)/shard_map/reduce_sum | solution.py:489
  7.2 0.0 copy-start.1
  7.2 0.0 copy-start.2
  7.3 1.7 %fusion.6 = f32[96,256]{1,0:T(8,128)S(1)} fusion(bf16[4096,256]{1,0:T(8,128)(2,1)S(1)} %copy-done, bf16[96,4096]{1,0:T(8,128)(2,1)} %param.10, f32[4096]{0:T(1024)} %param.11, f32[96]{0:T(128)S(1)} %add_rsqrt_fusion), kind=kOutput, calls=%fused_computation.37 | convolution fusion | flops 202899456 | bytes 2998656 | tf_op jit(solution)/shard_map/dot_general | solution.py:499
  9.0 0.1 reshape.91
  9.0 0.2 fusion.10
  9.3 0.1 maximum_bitcast_fusion.1
  9.4 2.1 %convolution_convert_fusion = bf16[96,256]{1,0:T(8,128)(2,1)S(1)} fusion(bf16[4096,256]{1,0:T(8,128)(2,1)} %param.14, bf16[96,4096]{1,0:T(8,128)(2,1)S(1)} %copy-done.1, f32[4096]{0:T(1024)S(1)} %copy-done.2, f32[96]{0:T(128)S(1)} %add_rsqrt_fusion), kind=kOutput, calls=%fused_computation.7 | convolution fusion | flops 202924032 | bytes 2949504 | tf_op jit(solution)/shard_map/dot_general | solution.py:504
  11.5 1.4 %copy.28 = bf16[1024,2,2,128]{3,0,2,1:T(8,128)(2,1)S(1)} copy(bf16[1024,2,2,128]{3,2,1,0:T(2,128)(2,1)} %param.16) | data formatting | bytes 2097152 | tf_op args[6]
  12.9 0.1 pad.8.clone
  13.0 0.3 maximum_bitcast_fusion
  13.3 1.1 %slice_bitcast_fusion = (bf16[2,1152,128]{2,1,0:T(8,128)(2,1)}, bf16[2,1152,128]{2,1,0:T(8,128)(2,1)}) fusion(bf16[2,2,1152,128]{3,2,1,0:T(8,128)(2,1)S(1)} %maximum_bitcast_fusion), kind=kLoop, calls=%fused_computation.8 | loop fusion | bytes 2359296 | tf_op jit(solution)/shard_map/squeeze | solution.py:542
  14.4 4.9 %convolution_bitcast_fusion = f32[12,8,8,128]{3,1,2,0:T(8,128)S(1)} fusion(bf16[4096,1024]{1,0:T(8,128)(2,1)} %param.12, bf16[96,4096]{1,0:T(8,128)(2,1)S(1)} %copy-done.1, f32[4096]{0:T(1024)S(1)} %copy-done.2, f32[96]{0:T(128)S(1)} %add_rsqrt_fusion), kind=kOutput, calls=%fused_computation.5 | convolution fusion | flops 806879232 | bytes 9585024 | tf_op jit(solution)/shard_map/dot_general | solution.py:492
  19.3 0.1 copy.34
  19.4 0.0 copy-start.3
  19.4 0.2 fusion.9
  19.6 0.2 subtract_convert_fusion
  19.8 0.8 pad_maximum_fusion
  20.6 0.1 reshape.92
  20.6 0.6 pad.4.row_pos
  21.3 76.9 %shard_map.113 = bf16[96,1024]{1,0:T(8,128)(2,1)} custom-call(bf16[2,384,128]{2,1,0:T(8,128)(2,1)} %bitcast.18, bf16[2,1152,128]{2,1,0:T(8,128)(2,1)} %get-tuple-element.11.key_in, bf16[2,1152,128]{2,1,0:T(8,128)(2,1)} %get-tuple-element.10.value_in, f32[1,2304]{1,0:T(1,128)} %broadcast_in_dim.15.key_pos, f32[32,128]{1,0:T(8,128)} %pad.4.row_pos, ...), custom_call_target="tpu_custom_call" | custom-call | tf_op jit(solution)/shard_map/pallas_call | solution.py:421
  98.2 0.7 copy.29
  98.9 1.6 %copy.44 = bf16[96,1024]{1,0:T(8,128)(2,1)} copy(bf16[96,1024]{1,0:T(8,128)(2,1)} %shard_map.113) | data formatting | bytes 393216
  (17 shorter events, 0.1 us)
Async XLA Ops:
  0.6 6.6 %copy-start = (bf16[4096,256]{1,0:T(8,128)(2,1)S(1)}, bf16[4096,256]{1,0:T(8,128)(2,1)}, u32[]{:S(2)}) copy-start(bf16[4096,256]{1,0:T(8,128)(2,1)} %param.13) | copy-start | bytes 6291460
  7.2 2.1 %copy-start.1 = (bf16[96,4096]{1,0:T(8,128)(2,1)S(1)}, bf16[96,4096]{1,0:T(8,128)(2,1)}, u32[]{:S(2)}) copy-start(bf16[96,4096]{1,0:T(8,128)(2,1)} %param.10) | copy-start | bytes 2359300
  7.2 2.1 %copy-start.2 = (f32[4096]{0:T(1024)S(1)}, f32[4096]{0:T(1024)}, u32[]{:S(2)}) copy-start(f32[4096]{0:T(1024)} %param.11) | copy-start | bytes 49156
  19.4 1.2 %copy-start.3 = (s32[3072]{0:T(1024)S(1)}, s32[3072]{0:T(1024)}, u32[]{:S(2)}) copy-start(s32[3072]{0:T(1024)} %param.17) | copy-start | bytes 36868

commit v2 on v1

v2 whole, which is shorter than its diff:
```python
import functools

import jax
import jax.numpy as jnp
from jax import lax
from jax.experimental import pallas as pl
from jax.experimental.pallas import tpu as pltpu
from jax.sharding import PartitionSpec as P

D = 4096
HEADS = 32
KV_HEADS = 8
HEAD_DIM = 128
PASSAGE = 4096
PASSAGES = 8
SIDE = 4
GROUP = HEADS // KV_HEADS
BLOCK = 1024
SEL = 96
FRESH = 128
HALF_KEYS = BLOCK + FRESH
KEYS = 2 * HALF_KEYS
ROWS = GROUP * SEL
FAR = 1.0e9
NEG = -1.0e30
LOG_SCALE = 1.4426950408889634 / HEAD_DIM**0.5
F32 = jnp.float32
BF16 = jnp.bfloat16
MESH = pl.DeviceIdType.MESH


def walk(i):
    return i + i // 2 - 2 * (i // 3)


def walk_last(i):
    return 2 - i + 3 * (i // 2) - 2 * (i // 3)


def line_of(t):
    first = walk(lax.rem(t, 4))
    return first + (walk_last(lax.rem(t, 4)) - first) * (t // 12)


def pack_rows(column):
    lane = lax.broadcasted_iota(jnp.int32, (SEL, 128), 1)
    total = jnp.zeros((SEL, 128), F32)
    for h in range(GROUP):
        total = jnp.where(lane == h, column[h * SEL : (h + 1) * SEL], total)
    square = jnp.concatenate([total, jnp.zeros((128 - SEL, 128), F32)], 0)
    return square.T[:8]


def unpack_rows(packed):
    square = jnp.concatenate([packed, jnp.zeros((120, 128), F32)], 0).T
    return jnp.concatenate(
        [jnp.broadcast_to(square[:SEL, h : h + 1], (SEL, 128)) for h in range(GROUP)], 0
    )


def merge(parts, stats):
    top = functools.reduce(jnp.maximum, stats)
    factors = [jnp.exp2(s - top) for s in stats]
    total = functools.reduce(jnp.add, factors)
    merged = sum(
        part.astype(F32) * unpack_rows(factor / total) for part, factor in zip(parts, factors)
    )
    return merged, top + jnp.log2(total)


def kernel(
    prompt_order,
    store_slot,
    hidden_in,
    gain,
    cosine,
    sine,
    row_pos,
    stored_in,
    w_query_in,
    w_key_in,
    w_value_in,
    w_out_in,
    out_ref,
    new_ref,
    hid,
    normed,
    wq,
    wkv,
    stored,
    wide,
    fresh,
    key_pos,
    qbuf,
    kbuf,
    vbuf,
    wbuf,
    scores,
    tops,
    part,
    stat,
    rb_part,
    rb_stat,
    mid,
    mid_stat,
    ra_part,
    ra_stat,
    ctx,
    zsend,
    zrelay,
    zrecv,
    local_sem,
    kv_ssem,
    kv_rsem,
    g_ssem,
    g_rsem,
    bp_ssem,
    bp_rsem,
    bs_ssem,
    bs_rsem,
    ap_ssem,
    ap_rsem,
    as_ssem,
    as_rsem,
    z_ssem,
    z_rsem,
):
    seq = lax.axis_index("seq")
    head = lax.axis_index("head")
    core = lax.rem(seq, 2)
    chip_x = lax.rem(seq // 2, SIDE)
    chip_y = seq // (2 * SIDE)

    def chip_seq(dx, dy):
        return (lax.rem(chip_y + dy, SIDE) * SIDE + lax.rem(chip_x + dx, SIDE)) * 2 + core

    def peer(g, da, db):
        return chip_seq(da, db) if g == 0 else chip_seq(db, da)

    def at(index):
        return (index, head)

    def above(dz):
        return (seq, lax.rem(head + dz, SIDE))

    other_seq = seq + 1 - 2 * core
    partner = (other_seq, head)

    barrier = pltpu.get_barrier_semaphore()
    others = [partner]
    for d in range(1, SIDE):
        others.append(at(chip_seq(d, 0)))
        others.append(at(chip_seq(0, d)))
    others += [above(1), above(3)]
    for other in others:
        pl.semaphore_signal(barrier, inc=1, device_id=other, device_id_type=MESH)

    load = pltpu.make_async_copy
    half_depth = D // 2
    own_hidden = load(hidden_in, hid, local_sem.at[0])
    own_stored = load(stored_in, stored, local_sem.at[1])
    q_loads = [
        [
            load(
                w_query_in.at[pl.ds(n * half_depth, half_depth), pl.ds(g * 512, 512)],
                wq.at[g, n],
                local_sem.at[2 + 2 * g + n],
            )
            for n in range(2)
        ]
        for g in range(2)
    ]
    kv_loads = [
        load(src, wkv.at[n], local_sem.at[6 + n]) for n, src in enumerate((w_key_in, w_value_in))
    ]
    weights = [
        load(w_out_in.at[:, pl.ds(n * 1024, 1024)], wbuf.at[n], local_sem.at[8 + n])
        for n in range(SIDE)
    ]
    own_hidden.start()
    q_loads[0][0].start()
    own_stored.start()
    q_loads[0][1].start()
    for copy in q_loads[1] + kv_loads + weights:
        copy.start()

    order = [store_slot[prompt_order[i]] for i in range(PASSAGES)]
    lanes = lax.broadcasted_iota(jnp.int32, (1, BLOCK), 1)
    short = lax.broadcasted_iota(jnp.int32, (1, FRESH), 1)
    per_passage = PASSAGE // BLOCK
    for n, device in enumerate((seq, other_seq)):
        place = jnp.int32(0)
        for i in range(PASSAGES):
            place = jnp.where(order[i] == device // per_passage, i, place)
        block = place * per_passage + lax.rem(device, per_passage)
        there = (block * BLOCK + lanes).astype(F32)
        replaced = jnp.broadcast_to(row_pos[pl.ds(block, 1), :], (128, 128)).T[:SEL, :1]
        gone = jnp.max(jnp.where(replaced == there, FAR, 0.0), 0, keepdims=True)
        key_pos[:, pl.ds(n * HALF_KEYS, BLOCK)] = there + gone
        key_pos[:, pl.ds(n * HALF_KEYS + BLOCK, FRESH)] = jnp.where(
            short < SEL, row_pos[pl.ds(device, 1), :], FAR
        )

    own_hidden.wait()
    widened = hid[...].astype(F32)
    mean = jnp.mean(widened * widened, -1, keepdims=True)
    normed[...] = (widened * lax.rsqrt(mean + 1e-05) * gain[...]).astype(BF16)

    own_stored.wait()
    wide[...] = stored[...].astype(F32)
    for n, buf in enumerate((kbuf, vbuf)):
        for g in range(2):
            rows = wide[pl.ds(2 * n + g, BLOCK, stride=4), :]
            buf[g, pl.ds(0, BLOCK), :] = rows.astype(BF16)
    pl.semaphore_wait(barrier, len(others))

    def to_partner(n, first, count):
        buf = (kbuf, vbuf)[n]
        index = 2 * n + (first > 0)
        return pltpu.make_async_remote_copy(
            src_ref=buf.at[:, pl.ds(first, count)],
            dst_ref=buf.at[:, pl.ds(HALF_KEYS + first, count)],
            send_sem=kv_ssem.at[index],
            recv_sem=kv_rsem.at[index],
            device_id=partner,
            device_id_type=MESH,
        )

    stored_copies = [to_partner(n, 0, BLOCK) for n in range(2)]
    fresh_copies = [to_partner(n, BLOCK, FRESH) for n in range(2)]
    for copy in stored_copies:
        copy.start()

    def whole(g, src, dst, sem, to):
        return pltpu.make_async_remote_copy(
            src_ref=qbuf.at[g, src],
            dst_ref=qbuf.at[g, dst],
            send_sem=g_ssem.at[g, sem],
            recv_sem=g_rsem.at[g, dst, 0],
            device_id=at(to),
            device_id_type=MESH,
        )

    def halved(g, src, dst, half, sem, to):
        rows = pl.ds(half * (ROWS // 2), ROWS // 2)
        return pltpu.make_async_remote_copy(
            src_ref=qbuf.at[g, src, rows],
            dst_ref=qbuf.at[g, dst, rows],
            send_sem=g_ssem.at[g, sem],
            recv_sem=g_rsem.at[g, dst, half],
            device_id=at(to),
            device_id_type=MESH,
        )

    def a_sends(g):
        return [whole(g, 0, 12, 0, peer(g, 1, 0)), whole(g, 0, 4, 1, peer(g, 3, 0))]

    def a_forward(g, da):
        if da == 3:
            return halved(g, 12, 8, 0, 2, peer(g, 1, 0))
        return halved(g, 4, 8, 1, 3, peer(g, 3, 0))

    def b_sends(g, da):
        return [
            whole(g, da * 4, da * 4 + 3, 4 + 4 * da, peer(g, 0, 1)),
            whole(g, da * 4, da * 4 + 1, 5 + 4 * da, peer(g, 0, 3)),
        ]

    def b_forwards(g, da):
        return [
            halved(g, da * 4 + 3, da * 4 + 2, 0, 6 + 4 * da, peer(g, 0, 1)),
            halved(g, da * 4 + 1, da * 4 + 2, 1, 7 + 4 * da, peer(g, 0, 3)),
        ]

    cos = cosine[...]
    sin = sine[...]

    def turned(x):
        return x * cos + pltpu.roll(x, HEAD_DIM // 2, 1) * sin

    for g in range(2):
        total = None
        for n in range(2):
            q_loads[g][n].wait()
            term = jnp.dot(
                normed[:, pl.ds(n * half_depth, half_depth)],
                wq[g, n],
                preferred_element_type=F32,
            )
            total = term if total is None else total + term
        for h in range(GROUP):
            qbuf[g, 0, pl.ds(h * SEL, SEL), :] = turned(total[:, h * 128 : (h + 1) * 128]).astype(
                BF16
            )
        for copy in a_sends(g):
            copy.start()
    for g in range(2):
        for copy in b_sends(g, 0):
            copy.start()

    for n, buf in enumerate((kbuf, vbuf)):
        kv_loads[n].wait()
        made = jnp.dot(normed[...], wkv[n], preferred_element_type=F32)
        for g in range(2):
            value = made[:, g * 128 : (g + 1) * 128]
            if n == 0:
                value = turned(value)
            buf[g, pl.ds(BLOCK, SEL), :] = value.astype(BF16)
            buf[g, pl.ds(BLOCK + SEL, FRESH - SEL), :] = jnp.zeros((FRESH - SEL, 128), BF16)
            fresh[pl.ds(2 * n + g, SEL, stride=4), :] = value
        fresh_copies[n].start()
    new_ref[...] = fresh[...].astype(BF16)

    def arrive(t, g):
        da = line_of(t)
        row = t // 4

        @pl.when(jnp.logical_or(t == 1, t == 2))
        def _():
            whole(g, 0, da * 4, 0, peer(g, 1, 0)).wait_recv()

        @pl.when(t == 1)
        def _():
            a_forward(g, 1).start()

        @pl.when(t == 2)
        def _():
            a_forward(g, 3).start()

        @pl.when(t == 3)
        def _():
            for half in range(2):
                halved(g, 0, 8, half, 0, peer(g, 1, 0)).wait_recv()

        @pl.when(row == 0)
        def _():
            for copy in b_sends(g, da):
                copy.start()

        @pl.when(row == 1)
        def _():
            for db in (1, 3):
                whole(g, 0, da * 4 + db, 0, peer(g, 1, 0)).wait_recv()
            for copy in b_forwards(g, da):
                copy.start()

        @pl.when(row == 2)
        def _():
            for half in range(2):
                halved(g, 0, da * 4 + 2, half, 0, peer(g, 1, 0)).wait_recv()

    def score(t, g):
        da = line_of(t)
        owner = peer(g, da, t // 4)
        s = lax.dot_general(
            qbuf[g, da * 4 + t // 4],
            kbuf[g],
            (((1,), (1,)), ((), ())),
            preferred_element_type=F32,
        )
        row = jnp.broadcast_to(row_pos[pl.ds(owner, 1), :], (128, 128)).T[:SEL, :1]
        pos = jnp.concatenate([row] * GROUP, 0)
        s = jnp.where(key_pos[...] <= pos, s, NEG)
        scores[g] = s
        tops[g] = jnp.broadcast_to(jnp.max(s, -1, keepdims=True), (ROWS, 128))

    def weigh(t, g):
        top = tops[g]
        e = jnp.exp2((scores[g] - top[:, :1]) * LOG_SCALE).astype(BF16)
        table = jnp.concatenate([vbuf[g], jnp.ones((KEYS, 128), BF16)], 1)
        summed = jnp.dot(e, table, preferred_element_type=F32)
        total = summed[:, 128:]
        part[g, t] = (summed[:, :128] / total).astype(BF16)
        stat[g, t] = pack_rows(top * LOG_SCALE + jnp.log2(total))

    def b_result(g, t, da, db):
        to = at(peer(g, 0, db))
        return [
            pltpu.make_async_remote_copy(
                src_ref=src.at[g, t],
                dst_ref=dst.at[g, da, db - 1],
                send_sem=ssem.at[g, da, db - 1],
                recv_sem=rsem.at[g, da, db - 1],
                device_id=to,
                device_id_type=MESH,
            )
            for src, dst, ssem, rsem in (
                (part, rb_part, bp_ssem, bp_rsem),
                (stat, rb_stat, bs_ssem, bs_rsem),
            )
        ]

    def a_result(g, da):
        to = at(peer(g, da, 0))
        return [
            pltpu.make_async_remote_copy(
                src_ref=src.at[g, da - 1],
                dst_ref=dst.at[g, da - 1],
                send_sem=ssem.at[g, da - 1],
                recv_sem=rsem.at[g, da - 1],
                device_id=to,
                device_id_type=MESH,
            )
            for src, dst, ssem, rsem in (
                (mid, ra_part, ap_ssem, ap_rsem),
                (mid_stat, ra_stat, as_ssem, as_rsem),
            )
        ]

    def line_sum(g, da, t):
        for db in range(1, SIDE):
            for copy in b_result(g, 0, da, db):
                copy.wait_recv()
        return merge(
            [part[g, t]] + [rb_part[g, da, n] for n in range(3)],
            [stat[g, t]] + [rb_stat[g, da, n] for n in range(3)],
        )

    def finish_line(da, t):
        for g in range(2):
            merged, logs = line_sum(g, da, t)
            mid[g, da - 1] = merged.astype(BF16)
            mid_stat[g, da - 1] = logs
            for copy in a_result(g, da):
                copy.start()

    def pass_on(t, g):
        for copy in b_result(g, t, line_of(t), t // 4):
            copy.start()

    for copy in stored_copies + fresh_copies:
        copy.wait_recv()
    score(0, 0)

    def step(t, carry):
        @pl.when(t > 0)
        def _():
            arrive(t, 1)

        @pl.when(t == 14)
        def _():
            finish_line(2, 3)

        score(t, 1)
        weigh(t, 0)

        @pl.when(t >= 4)
        def _():
            pass_on(t, 0)

        arrive(t + 1, 0)
        score(t + 1, 0)
        weigh(t, 1)

        @pl.when(t >= 4)
        def _():
            pass_on(t, 1)

        return carry

    lax.fori_loop(0, 15, step, 0)
    score(15, 1)
    weigh(15, 0)
    pass_on(15, 0)
    finish_line(1, 1)
    weigh(15, 1)
    pass_on(15, 1)
    finish_line(3, 2)
    for g in range(2):
        merged, logs = line_sum(g, 0, 0)
        part[g, 0] = merged.astype(BF16)
        stat[g, 0] = logs
    for g in range(2):
        for da in (2, 1, 3):
            for copy in a_result(g, da):
                copy.wait_recv()
        merged, _ = merge(
            [part[g, 0]] + [ra_part[g, n] for n in range(3)],
            [stat[g, 0]] + [ra_stat[g, n] for n in range(3)],
        )
        for h in range(GROUP):
            ctx[:, pl.ds((g * GROUP + h) * 128, 128)] = merged[h * SEL : (h + 1) * SEL].astype(BF16)

    for copy in weights:
        copy.wait()

    lower = pl.ds(0, SEL // 2)
    upper = pl.ds(SEL // 2, SEL // 2)

    def z_copy(index, src, dst, dz):
        return pltpu.make_async_remote_copy(
            src_ref=src,
            dst_ref=dst,
            send_sem=z_ssem.at[index],
            recv_sem=z_rsem.at[index],
            device_id=above(dz),
            device_id_type=MESH,
        )

    def projected(dz):
        return jnp.dot(ctx[...], wbuf[lax.rem(head + dz, SIDE)], preferred_element_type=F32)

    up_far = z_copy(0, zsend.at[0, lower], zrelay.at[0], 1)
    down_far = z_copy(1, zsend.at[0, upper], zrelay.at[1], 3)
    up_free = z_copy(2, zsend.at[1, upper], zrecv.at[0, upper], 1)
    up_sum = z_copy(3, zsend.at[1, lower], zrecv.at[0, lower], 1)
    down_free = z_copy(4, zsend.at[2, lower], zrecv.at[1, lower], 3)
    down_sum = z_copy(5, zsend.at[2, upper], zrecv.at[1, upper], 3)
    zsend[0] = projected(2).astype(BF16)
    up_far.start()
    down_far.start()
    up = projected(1)
    zsend[1, upper] = up[SEL // 2 :].astype(BF16)
    up_free.start()
    up_far.wait_recv()
    zsend[1, lower] = (up[: SEL // 2] + zrelay[0].astype(F32)).astype(BF16)
    up_sum.start()
    down = projected(3)
    zsend[2, lower] = down[: SEL // 2].astype(BF16)
    down_free.start()
    down_far.wait_recv()
    zsend[2, upper] = (down[SEL // 2 :] + zrelay[1].astype(F32)).astype(BF16)
    down_sum.start()
    total = projected(0)
    for copy in (up_free, up_sum, down_free, down_sum):
        copy.wait_recv()
    out_ref[...] = (total + zrecv[0].astype(F32) + zrecv[1].astype(F32)).astype(BF16)

    for copy in stored_copies + fresh_copies:
        copy.wait_send()
    for g in range(2):
        for copy in a_sends(g) + [a_forward(g, 3), a_forward(g, 1)]:
            copy.wait_send()
        for da in range(4):
            for copy in b_sends(g, da) + b_forwards(g, da):
                copy.wait_send()
            for db in range(1, 4):
                for copy in b_result(g, 0, da, db):
                    copy.wait_send()
        for da in range(1, 4):
            for copy in a_result(g, da):
                copy.wait_send()
    for copy in (up_far, down_far, up_free, up_sum, down_free, down_sum):
        copy.wait_send()


def attend(*operands):
    vmem = pl.BlockSpec(memory_space=pltpu.VMEM)
    smem = pl.BlockSpec(memory_space=pltpu.SMEM)
    hbm = pl.BlockSpec(memory_space=pl.ANY)
    dma = pltpu.SemaphoreType.DMA
    return pl.pallas_call(
        kernel,
        out_shape=(
            jax.ShapeDtypeStruct((SEL, 1024), BF16),
            jax.ShapeDtypeStruct((4 * SEL, 128), BF16),
        ),
        in_specs=[smem, smem, hbm, vmem, vmem, vmem, vmem, hbm, hbm, hbm, hbm, hbm],
        out_specs=(vmem, vmem),
        scratch_shapes=[
            pltpu.VMEM((SEL, D), BF16),
            pltpu.VMEM((SEL, D), BF16),
            pltpu.VMEM((2, 2, D // 2, 512), BF16),
            pltpu.VMEM((2, D, 256), BF16),
            pltpu.VMEM((4 * BLOCK, 128), BF16),
            pltpu.VMEM((4 * BLOCK, 128), F32),
            pltpu.VMEM((4 * SEL, 128), F32),
            pltpu.VMEM((1, KEYS), F32),
            pltpu.VMEM((2, 16, ROWS, 128), BF16),
            pltpu.VMEM((2, KEYS, 128), BF16),
            pltpu.VMEM((2, KEYS, 128), BF16),
            pltpu.VMEM((SIDE, 1024, 1024), BF16),
            pltpu.VMEM((2, ROWS, KEYS), F32),
            pltpu.VMEM((2, ROWS, 128), F32),
            pltpu.VMEM((2, 16, ROWS, 128), BF16),
            pltpu.VMEM((2, 16, 8, 128), F32),
            pltpu.VMEM((2, 4, 3, ROWS, 128), BF16),
            pltpu.VMEM((2, 4, 3, 8, 128), F32),
            pltpu.VMEM((2, 3, ROWS, 128), BF16),
            pltpu.VMEM((2, 3, 8, 128), F32),
            pltpu.VMEM((2, 3, ROWS, 128), BF16),
            pltpu.VMEM((2, 3, 8, 128), F32),
            pltpu.VMEM((SEL, 1024), BF16),
            pltpu.VMEM((3, SEL, 1024), BF16),
            pltpu.VMEM((2, SEL // 2, 1024), BF16),
            pltpu.VMEM((2, SEL, 1024), BF16),
            dma((12,)),
            dma((4,)),
            dma((4,)),
            dma((2, 20)),
            dma((2, 16, 2)),
            dma((2, 4, 3)),
            dma((2, 4, 3)),
            dma((2, 4, 3)),
            dma((2, 4, 3)),
            dma((2, 3)),
            dma((2, 3)),
            dma((2, 3)),
            dma((2, 3)),
            dma((6,)),
            dma((6,)),
        ],
        compiler_params=pltpu.CompilerParams(
            collective_id=0, has_side_effects=True, vmem_limit_bytes=64_000_000
        ),
    )(*operands)


def body(
    hidden, norm_gain, w_query, w_key, w_value, w_out, stored_kv, selected, prompt_order, store_slot
):
    positions = lax.dynamic_slice_in_dim(selected, lax.axis_index("seq") * SEL, SEL)
    half = HEAD_DIM // 2
    freq = 500000.0 ** (-(jnp.arange(half, dtype=jnp.float32) * 2.0 / HEAD_DIM))
    angle = positions.astype(jnp.float32)[:, None] * freq[None, :]
    cosine = jnp.cos(angle)
    sine = jnp.sin(angle)
    row_pos = jnp.pad(selected.astype(F32).reshape(-1, SEL), ((0, 0), (0, 128 - SEL)))
    attn_out, new_kv = attend(
        prompt_order,
        store_slot,
        hidden,
        norm_gain[None],
        jnp.concatenate([cosine, cosine], 1),
        jnp.concatenate([-sine, sine], 1),
        row_pos,
        stored_kv.reshape(-1, HEAD_DIM),
        w_query,
        w_key,
        w_value,
        w_out,
    )
    return (attn_out, new_kv.reshape(SEL, 2, 2, HEAD_DIM))


def solution(mesh):
    in_specs = (
        P("seq", None),
        P(),
        P(None, "head"),
        P(None, "head"),
        P(None, "head"),
        P("head", None),
        P("seq", None, "head", None),
        P(),
        P(),
        P(),
    )
    out_specs = (P("seq", "head"), P("seq", None, "head", None))
    return jax.shard_map(body, mesh=mesh, in_specs=in_specs, out_specs=out_specs, check_vma=False)
```

time: 101 us -> 87.5 us (0.87)
  matrix products: 8.78 us -> 0 us
  other arithmetic: 5.84 us -> 2.49 us
  Pallas kernels: 76.9 us -> 79.9 us
  local copies, waits for them, and re-layouts: 6.77 us -> 3.9 us
  between operations: 2.23 us -> 0.65 us
    dot_general x3 -> x0, matrix products: 8.78 us -> none  [the longest x1 4.94 us: body(): jnp.dot(normed, w_query, preferred_element_type=jnp.float32)]
    reduce_sum x4 -> x0, other arithmetic: 3.1 us -> none  [the longest x1 1.39 us: body(): jnp.mean(widened * widened, -1, keepdims=True) + 1e-05]
    pallas_call x1, Pallas kernels: 76.9 us -> 79.9 us  [attend(): pl.pallas_call(kernel, out_shape=(jax.ShapeDtypeStruct((SEL, 1024), BF16)...]
    squeeze x1 -> x0, local copies, waits for them, and re-layouts: 1.09 us -> none  [body(): attn_out = attend(query, both[0], both[1], key_pos, row_pos, w_out)]
    unnamed x12 -> x2, local copies, waits for them, and re-layouts: 3.8 us -> 3.22 us
where the time goes in v2:
time: 87.5 us; the launch traced here: 87 us
  Pallas kernels  79.9 us (91%)
  local copies, waits for them, and re-layouts  3.9 us (4%)
  other arithmetic  2.49 us (3%)
    pallas_call x1, Pallas kernels, attend(): pl.pallas_call(kernel, out_shape=(jax.ShapeDtypeStruct((SEL, 1024), BF16)...  79.9 us
    unnamed x2, local copies, waits for them, and re-layouts  3.22 us

profile of v2, /device:TPU:0, one launch (start us, length us, event | category | flops | bytes accessed | tf_op | source)
XLA Modules:
  0.0 87.0 jit_solution(1865611163649005820)
XLA Ops:
  0.6 0.8 dynamic-slice_convert_fusion
  1.4 0.7 convert_element_type.9
  2.1 0.1 reshape.20
  2.2 0.6 pad.4.row_pos
  2.8 0.2 fusion
  3.1 0.7 pad_maximum_fusion
  3.8 79.9 %shard_map.113 = (bf16[96,1024]{1,0:T(8,128)(2,1)}, bf16[384,128]{1,0:T(8,128)(2,1)}) custom-call(s32[8]{0:T(128)} %prompt_order.1, s32[8]{0:T(128)} %store_slot.1, bf16[96,4096]{1,0:T(8,128)(2,1)} %hidden_in.1, f32[1,4096]{1,0:T(1,128)} %bitcast.5, f32[96,128]{1,0:T(8,128)} %get-tuple-element.9.cosine, f32[96,128]{1,0:T(8,128)} %get-tuple-element.10.sine, ...), custom_call_target="tpu_custom_call" | custom-call | tf_op jit(solution)/shard_map/pallas_call | solution.py:552
  83.8 1.6 %copy.14 = bf16[96,1024]{1,0:T(8,128)(2,1)} copy(bf16[96,1024]{1,0:T(8,128)(2,1)} %get-tuple-element.13) | data formatting | bytes 393216
  85.4 1.6 %copy.15 = bf16[96,2,2,128]{3,2,1,0:T(2,128)(2,1)} copy(bf16[96,2,2,128]{3,2,1,0:T(2,128)(2,1)} %bitcast.4) | data formatting | bytes 196608
  (1 shorter events, 0.0 us)

commit v3 on v2

--- a/solution.py
+++ b/solution.py
@@ -29,17 +29,20 @@
 MESH = pl.DeviceIdType.MESH
 
 
-def walk(i):
-    return i + i // 2 - 2 * (i // 3)
-
-
-def walk_last(i):
-    return 2 - i + 3 * (i // 2) - 2 * (i // 3)
-
-
-def line_of(t):
-    first = walk(lax.rem(t, 4))
-    return first + (walk_last(lax.rem(t, 4)) - first) * (t // 12)
+WALK = (
+    (0, 1), (0, 3), (0, 2), (1, 1), (1, 3), (3, 1), (3, 3), (1, 2),
+    (3, 2), (2, 1), (2, 3), (2, 2), (1, 0), (2, 0), (3, 0), (0, 0),
+)
+OWN = {da: t for t, (da, db) in enumerate(WALK) if db == 0}
+
+
+def offset(t, axis):
+    if isinstance(t, int):
+        return WALK[t][axis]
+    found = jnp.int32(0)
+    for n, pair in enumerate(WALK):
+        found = jnp.where(t == n, pair[axis], found)
+    return found
 
 
 def pack_rows(column):
@@ -69,13 +72,12 @@
 
 
 def kernel(
-    prompt_order,
-    store_slot,
+    order_in,
+    slot_in,
     hidden_in,
-    gain,
-    cosine,
-    sine,
-    row_pos,
+    gain_in,
+    freq_in,
+    selected_in,
     stored_in,
     w_query_in,
     w_key_in,
@@ -83,6 +85,12 @@
     w_out_in,
     out_ref,
     new_ref,
+    prompt_order,
+    store_slot,
+    gain,
+    freq,
+    listed,
+    row_pos,
     hid,
     normed,
     wq,
@@ -177,12 +185,48 @@
         load(w_out_in.at[:, pl.ds(n * 1024, 1024)], wbuf.at[n], local_sem.at[8 + n])
         for n in range(SIDE)
     ]
+    small = [
+        load(src, dst, local_sem.at[12 + n])
+        for n, (src, dst) in enumerate(
+            (
+                (selected_in, listed),
+                (freq_in, freq),
+                (gain_in, gain),
+                (order_in, prompt_order),
+                (slot_in, store_slot),
+            )
+        )
+    ]
+    for copy in small:
+        copy.start()
     own_hidden.start()
     q_loads[0][0].start()
     own_stored.start()
     q_loads[0][1].start()
     for copy in q_loads[1] + kv_loads + weights:
         copy.start()
+
+    for copy in small:
+        copy.wait()
+
+    wide[pl.ds(0, 24), :] = listed[...].astype(F32)
+    thirds = [wide[pl.ds(n, 8, stride=3), :] for n in range(3)]
+    lane = lax.broadcasted_iota(jnp.int32, (8, 128), 1)
+    roll = pltpu.roll
+    for n, rows in enumerate(
+        (
+            thirds[0],
+            jnp.where(lane < 32, roll(thirds[0], 32, 1), roll(thirds[1], 32, 1)),
+            jnp.where(lane < 64, roll(thirds[1], 64, 1), roll(thirds[2], 64, 1)),
+            roll(thirds[2], 96, 1),
+        )
+    ):
+        row_pos[pl.ds(n, 8, stride=4), :] = rows
+
+    angle = jnp.broadcast_to(row_pos[pl.ds(seq, 1), :], (128, 128)).T[:SEL] * freq[...]
+    cos = jnp.cos(angle)
+    sin = jnp.sin(angle)
+    sin = jnp.where(lax.broadcasted_iota(jnp.int32, (SEL, 128), 1) < HEAD_DIM // 2, -sin, sin)
 
     order = [store_slot[prompt_order[i]] for i in range(PASSAGES)]
     lanes = lax.broadcasted_iota(jnp.int32, (1, BLOCK), 1)
@@ -272,9 +316,6 @@
             halved(g, da * 4 + 1, da * 4 + 2, 1, 7 + 4 * da, peer(g, 0, 3)),
         ]
 
-    cos = cosine[...]
-    sin = sine[...]
-
     def turned(x):
         return x * cos + pltpu.roll(x, HEAD_DIM // 2, 1) * sin
 
@@ -292,10 +333,7 @@
             qbuf[g, 0, pl.ds(h * SEL, SEL), :] = turned(total[:, h * 128 : (h + 1) * 128]).astype(
                 BF16
             )
-        for copy in a_sends(g):
-            copy.start()
-    for g in range(2):
-        for copy in b_sends(g, 0):
+        for copy in a_sends(g) + b_sends(g, 0):
             copy.start()
 
     for n, buf in enumerate((kbuf, vbuf)):
@@ -311,49 +349,53 @@
         fresh_copies[n].start()
     new_ref[...] = fresh[...].astype(BF16)
 
+    def full(g, da, db):
+        whole(g, 0, da * 4 + db, 0, peer(g, 1, 0)).wait_recv()
+
+    def both_halves(g, da, db):
+        for half in range(2):
+            halved(g, 0, da * 4 + db, half, 0, peer(g, 1, 0)).wait_recv()
+
     def arrive(t, g):
-        da = line_of(t)
-        row = t // 4
-
-        @pl.when(jnp.logical_or(t == 1, t == 2))
+        @pl.when(t == 0)
         def _():
-            whole(g, 0, da * 4, 0, peer(g, 1, 0)).wait_recv()
-
-        @pl.when(t == 1)
-        def _():
-            a_forward(g, 1).start()
+            for db in (1, 3):
+                full(g, 0, db)
+            for copy in b_forwards(g, 0):
+                copy.start()
+            for da in (1, 3):
+                full(g, da, 0)
+                a_forward(g, da).start()
+            for copy in b_sends(g, 1) + b_sends(g, 3):
+                copy.start()
 
         @pl.when(t == 2)
         def _():
-            a_forward(g, 3).start()
-
-        @pl.when(t == 3)
-        def _():
-            for half in range(2):
-                halved(g, 0, 8, half, 0, peer(g, 1, 0)).wait_recv()
-
-        @pl.when(row == 0)
-        def _():
-            for copy in b_sends(g, da):
+            both_halves(g, 0, 2)
+            both_halves(g, 2, 0)
+            for copy in b_sends(g, 2):
                 copy.start()
 
-        @pl.when(row == 1)
-        def _():
-            for db in (1, 3):
-                whole(g, 0, da * 4 + db, 0, peer(g, 1, 0)).wait_recv()
-            for copy in b_forwards(g, da):
-                copy.start()
-
-        @pl.when(row == 2)
-        def _():
-            for half in range(2):
-                halved(g, 0, da * 4 + 2, half, 0, peer(g, 1, 0)).wait_recv()
+        for first, da in ((3, 1), (5, 3), (9, 2)):
+
+            @pl.when(t == first)
+            def _(da=da):
+                for db in (1, 3):
+                    full(g, da, db)
+                for copy in b_forwards(g, da):
+                    copy.start()
+
+        for last, da in ((7, 1), (8, 3), (11, 2)):
+
+            @pl.when(t == last)
+            def _(da=da):
+                both_halves(g, da, 2)
 
     def score(t, g):
-        da = line_of(t)
-        owner = peer(g, da, t // 4)
+        da, db = offset(t, 0), offset(t, 1)
+        owner = peer(g, da, db)
         s = lax.dot_general(
-            qbuf[g, da * 4 + t // 4],
+            qbuf[g, da * 4 + db],
             kbuf[g],
             (((1,), (1,)), ((), ())),
             preferred_element_type=F32,
@@ -362,10 +404,12 @@
         pos = jnp.concatenate([row] * GROUP, 0)
         s = jnp.where(key_pos[...] <= pos, s, NEG)
         scores[g] = s
-        tops[g] = jnp.broadcast_to(jnp.max(s, -1, keepdims=True), (ROWS, 128))
+        tops[g] = functools.reduce(
+            jnp.maximum, [s[:, n * 128 : (n + 1) * 128] for n in range(KEYS // 128)]
+        )
 
     def weigh(t, g):
-        top = tops[g]
+        top = jnp.broadcast_to(jnp.max(tops[g], -1, keepdims=True), (ROWS, 128))
         e = jnp.exp2((scores[g] - top[:, :1]) * LOG_SCALE).astype(BF16)
         table = jnp.concatenate([vbuf[g], jnp.ones((KEYS, 128), BF16)], 1)
         summed = jnp.dot(e, table, preferred_element_type=F32)
@@ -407,76 +451,64 @@
             )
         ]
 
-    def line_sum(g, da, t):
+    def line(g, da):
         for db in range(1, SIDE):
             for copy in b_result(g, 0, da, db):
                 copy.wait_recv()
-        return merge(
+        t = OWN[da]
+        return (
             [part[g, t]] + [rb_part[g, da, n] for n in range(3)],
             [stat[g, t]] + [rb_stat[g, da, n] for n in range(3)],
         )
 
-    def finish_line(da, t):
+    def finish_line(da):
         for g in range(2):
-            merged, logs = line_sum(g, da, t)
+            merged, logs = merge(*line(g, da))
             mid[g, da - 1] = merged.astype(BF16)
             mid_stat[g, da - 1] = logs
             for copy in a_result(g, da):
                 copy.start()
 
     def pass_on(t, g):
-        for copy in b_result(g, t, line_of(t), t // 4):
-            copy.start()
+        @pl.when(t < 12)
+        def _():
+            for copy in b_result(g, t, offset(t, 0), offset(t, 1)):
+                copy.start()
 
     for copy in stored_copies + fresh_copies:
         copy.wait_recv()
+    arrive(jnp.int32(0), 0)
     score(0, 0)
 
     def step(t, carry):
-        @pl.when(t > 0)
-        def _():
-            arrive(t, 1)
-
-        @pl.when(t == 14)
-        def _():
-            finish_line(2, 3)
+        arrive(t, 1)
+        for da in (1, 2):
+
+            @pl.when(t == OWN[da] + 1)
+            def _(da=da):
+                finish_line(da)
 
         score(t, 1)
         weigh(t, 0)
-
-        @pl.when(t >= 4)
-        def _():
-            pass_on(t, 0)
-
+        pass_on(t, 0)
         arrive(t + 1, 0)
         score(t + 1, 0)
         weigh(t, 1)
-
-        @pl.when(t >= 4)
-        def _():
-            pass_on(t, 1)
-
+        pass_on(t, 1)
         return carry
 
     lax.fori_loop(0, 15, step, 0)
+    finish_line(3)
     score(15, 1)
     weigh(15, 0)
-    pass_on(15, 0)
-    finish_line(1, 1)
     weigh(15, 1)
-    pass_on(15, 1)
-    finish_line(3, 2)
     for g in range(2):
-        merged, logs = line_sum(g, 0, 0)
-        part[g, 0] = merged.astype(BF16)
-        stat[g, 0] = logs
-    for g in range(2):
-        for da in (2, 1, 3):
+        parts, stats = line(g, 0)
+        for da in (1, 2, 3):
             for copy in a_result(g, da):
                 copy.wait_recv()
         merged, _ = merge(
-            [part[g, 0]] + [ra_part[g, n] for n in range(3)],
-            [stat[g, 0]] + [ra_stat[g, n] for n in range(3)],
+            parts + [ra_part[g, n] for n in range(3)], stats + [ra_stat[g, n] for n in range(3)]
         )
         for h in range(GROUP):
             ctx[:, pl.ds((g * GROUP + h) * 128, 128)] = merged[h * SEL : (h + 1) * SEL].astype(BF16)
@@ -546,18 +578,23 @@
 
 def attend(*operands):
     vmem = pl.BlockSpec(memory_space=pltpu.VMEM)
-    smem = pl.BlockSpec(memory_space=pltpu.SMEM)
     hbm = pl.BlockSpec(memory_space=pl.ANY)
     dma = pltpu.SemaphoreType.DMA
     return pl.pallas_call(
         kernel,
         out_shape=(
-            jax.ShapeDtypeStruct((SEL, 1024), BF16),
-            jax.ShapeDtypeStruct((4 * SEL, 128), BF16),
+            pltpu.VMEM((SEL, 1024), BF16),
+            pltpu.VMEM((4 * SEL, 128), BF16),
         ),
-        in_specs=[smem, smem, hbm, vmem, vmem, vmem, vmem, hbm, hbm, hbm, hbm, hbm],
+        in_specs=[hbm] * 11,
         out_specs=(vmem, vmem),
         scratch_shapes=[
+            pltpu.SMEM((PASSAGES,), jnp.int32),
+            pltpu.SMEM((PASSAGES,), jnp.int32),
+            pltpu.VMEM((1, D), F32),
+            pltpu.VMEM((1, 128), F32),
+            pltpu.VMEM((24, 128), jnp.int32),
+            pltpu.VMEM((32, 128), F32),
             pltpu.VMEM((SEL, D), BF16),
             pltpu.VMEM((SEL, D), BF16),
             pltpu.VMEM((2, 2, D // 2, 512), BF16),
@@ -584,7 +621,7 @@
             pltpu.VMEM((3, SEL, 1024), BF16),
             pltpu.VMEM((2, SEL // 2, 1024), BF16),
             pltpu.VMEM((2, SEL, 1024), BF16),
-            dma((12,)),
+            dma((17,)),
             dma((4,)),
             dma((4,)),
             dma((2, 20)),
@@ -609,21 +646,16 @@
 def body(
     hidden, norm_gain, w_query, w_key, w_value, w_out, stored_kv, selected, prompt_order, store_slot
 ):
-    positions = lax.dynamic_slice_in_dim(selected, lax.axis_index("seq") * SEL, SEL)
     half = HEAD_DIM // 2
-    freq = 500000.0 ** (-(jnp.arange(half, dtype=jnp.float32) * 2.0 / HEAD_DIM))
-    angle = positions.astype(jnp.float32)[:, None] * freq[None, :]
-    cosine = jnp.cos(angle)
-    sine = jnp.sin(angle)
-    row_pos = jnp.pad(selected.astype(F32).reshape(-1, SEL), ((0, 0), (0, 128 - SEL)))
+    index = jnp.arange(HEAD_DIM, dtype=jnp.int32) % half
+    freq = 500000.0 ** (-(index.astype(F32) * 2.0 / HEAD_DIM))
     attn_out, new_kv = attend(
         prompt_order,
         store_slot,
         hidden,
         norm_gain[None],
-        jnp.concatenate([cosine, cosine], 1),
-        jnp.concatenate([-sine, sine], 1),
-        row_pos,
+        freq[None],
+        selected.reshape(24, 128),
         stored_kv.reshape(-1, HEAD_DIM),
         w_query,
         w_key,

time: 87.5 us -> 78.6 us (0.90)
  Pallas kernels: 79.9 us -> 75.8 us
  local copies, waits for them, and re-layouts: 3.9 us -> 1.32 us
  other arithmetic: 2.49 us -> 0.52 us
    pallas_call x1, Pallas kernels: 79.9 us -> 75.8 us  [attend(): pl.pallas_call(kernel, out_shape=(pltpu.VMEM((SEL, 1024), BF16), pltpu.VM...]
    unnamed x2, local copies, waits for them, and re-layouts: 3.22 us -> 1.32 us
    convert_element_type x2 -> x0, other arithmetic: 1.49 us -> none  [the longest x1 0.78 us: body(): angle = positions.astype(jnp.float32)[:, None] * freq[None, :]]
where the time goes in v3:
time: 78.6 us; the launch traced here: 78.3 us
  Pallas kernels  75.8 us (96%)
  local copies, waits for them, and re-layouts  1.32 us (2%)
    pallas_call x1, Pallas kernels, attend(): pl.pallas_call(kernel, out_shape=(pltpu.VMEM((SEL, 1024), BF16), pltpu.VM...  75.8 us

profile of v3, /device:TPU:0, one launch (start us, length us, event | category | flops | bytes accessed | tf_op | source)
XLA Modules:
  0.0 78.3 jit_solution(1879787113389373664)
XLA Ops:
  0.6 0.5 fusion.3.freq_in
  1.2 75.8 %shard_map.113 = (bf16[96,1024]{1,0:T(8,128)(2,1)S(1)}, bf16[384,128]{1,0:T(8,128)(2,1)S(1)}) custom-call(s32[8]{0:T(128)} %order_in.1, s32[8]{0:T(128)} %slot_in.1, bf16[96,4096]{1,0:T(8,128)(2,1)} %hidden_in.1, f32[1,4096]{1,0:T(1,128)} %bitcast.6, f32[1,128]{1,0:T(1,128)} %fusion.3.freq_in, s32[24,128]{1,0:T(8,128)} %bitcast.7, ...), custom_call_target="tpu_custom_call" | custom-call | tf_op jit(solution)/shard_map/pallas_call | solution.py:583
  76.9 0.7 copy.14
  77.6 0.6 copy.15

commit v4 on v3

--- a/solution.py
+++ b/solution.py
@@ -18,10 +18,8 @@
 BLOCK = 1024
 SEL = 96
 FRESH = 128
-HALF_KEYS = BLOCK + FRESH
-KEYS = 2 * HALF_KEYS
+KEYS = 2 * BLOCK
 ROWS = GROUP * SEL
-FAR = 1.0e9
 NEG = -1.0e30
 LOG_SCALE = 1.4426950408889634 / HEAD_DIM**0.5
 F32 = jnp.float32
@@ -98,6 +96,7 @@
     stored,
     wide,
     fresh,
+    made_kv,
     key_pos,
     qbuf,
     kbuf,
@@ -200,10 +199,7 @@
     for copy in small:
         copy.start()
     own_hidden.start()
-    q_loads[0][0].start()
-    own_stored.start()
-    q_loads[0][1].start()
-    for copy in q_loads[1] + kv_loads + weights:
+    for copy in q_loads[0]:
         copy.start()
 
     for copy in small:
@@ -230,50 +226,42 @@
 
     order = [store_slot[prompt_order[i]] for i in range(PASSAGES)]
     lanes = lax.broadcasted_iota(jnp.int32, (1, BLOCK), 1)
-    short = lax.broadcasted_iota(jnp.int32, (1, FRESH), 1)
     per_passage = PASSAGE // BLOCK
+    blocks = []
     for n, device in enumerate((seq, other_seq)):
         place = jnp.int32(0)
         for i in range(PASSAGES):
             place = jnp.where(order[i] == device // per_passage, i, place)
         block = place * per_passage + lax.rem(device, per_passage)
+        blocks.append(block)
         there = (block * BLOCK + lanes).astype(F32)
         replaced = jnp.broadcast_to(row_pos[pl.ds(block, 1), :], (128, 128)).T[:SEL, :1]
-        gone = jnp.max(jnp.where(replaced == there, FAR, 0.0), 0, keepdims=True)
-        key_pos[:, pl.ds(n * HALF_KEYS, BLOCK)] = there + gone
-        key_pos[:, pl.ds(n * HALF_KEYS + BLOCK, FRESH)] = jnp.where(
-            short < SEL, row_pos[pl.ds(device, 1), :], FAR
-        )
+        made = jnp.broadcast_to(row_pos[pl.ds(device, 1), :], (128, 128)).T[:SEL, :1]
+        put = jnp.sum(jnp.where(replaced == there, made + 1.0, 0.0), 0, keepdims=True)
+        key_pos[:, pl.ds(n * BLOCK, BLOCK)] = jnp.where(put > 0.0, put - 1.0, there)
 
     own_hidden.wait()
+    own_stored.start()
+    q_loads[1][0].start()
     widened = hid[...].astype(F32)
     mean = jnp.mean(widened * widened, -1, keepdims=True)
     normed[...] = (widened * lax.rsqrt(mean + 1e-05) * gain[...]).astype(BF16)
 
-    own_stored.wait()
-    wide[...] = stored[...].astype(F32)
-    for n, buf in enumerate((kbuf, vbuf)):
-        for g in range(2):
-            rows = wide[pl.ds(2 * n + g, BLOCK, stride=4), :]
-            buf[g, pl.ds(0, BLOCK), :] = rows.astype(BF16)
-    pl.semaphore_wait(barrier, len(others))
-
-    def to_partner(n, first, count):
-        buf = (kbuf, vbuf)[n]
-        index = 2 * n + (first > 0)
+    def to_partner(index, src, dst):
         return pltpu.make_async_remote_copy(
-            src_ref=buf.at[:, pl.ds(first, count)],
-            dst_ref=buf.at[:, pl.ds(HALF_KEYS + first, count)],
+            src_ref=src,
+            dst_ref=dst,
             send_sem=kv_ssem.at[index],
             recv_sem=kv_rsem.at[index],
             device_id=partner,
             device_id_type=MESH,
         )
 
-    stored_copies = [to_partner(n, 0, BLOCK) for n in range(2)]
-    fresh_copies = [to_partner(n, BLOCK, FRESH) for n in range(2)]
-    for copy in stored_copies:
-        copy.start()
+    stored_copies = [
+        to_partner(n, buf.at[:, pl.ds(0, BLOCK)], buf.at[:, pl.ds(BLOCK, BLOCK)])
+        for n, buf in enumerate((kbuf, vbuf))
+    ]
+    fresh_copies = [to_partner(2 + n, made_kv.at[0, n], made_kv.at[1, n]) for n in range(2)]
 
     def whole(g, src, dst, sem, to):
         return pltpu.make_async_remote_copy(
@@ -319,10 +307,14 @@
     def turned(x):
         return x * cos + pltpu.roll(x, HEAD_DIM // 2, 1) * sin
 
+    pl.semaphore_wait(barrier, len(others))
+    later = {(0, 0): q_loads[1][1], (0, 1): kv_loads[0], (1, 0): kv_loads[1]}
     for g in range(2):
         total = None
         for n in range(2):
             q_loads[g][n].wait()
+            if (g, n) in later:
+                later[g, n].start()
             term = jnp.dot(
                 normed[:, pl.ds(n * half_depth, half_depth)],
                 wq[g, n],
@@ -335,18 +327,52 @@
             )
         for copy in a_sends(g) + b_sends(g, 0):
             copy.start()
-
-    for n, buf in enumerate((kbuf, vbuf)):
+        if g == 0:
+            own_stored.wait()
+            wide[...] = stored[...].astype(F32)
+            for n, buf in enumerate((kbuf, vbuf)):
+                for k in range(2):
+                    rows = wide[pl.ds(2 * n + k, BLOCK, stride=4), :]
+                    buf[k, pl.ds(0, BLOCK), :] = rows.astype(BF16)
+                stored_copies[n].start()
+
+    for n in range(2):
         kv_loads[n].wait()
         made = jnp.dot(normed[...], wkv[n], preferred_element_type=F32)
+        made_kv[0, n, pl.ds(SEL, FRESH - SEL), :] = jnp.zeros((FRESH - SEL, 256), BF16)
         for g in range(2):
             value = made[:, g * 128 : (g + 1) * 128]
             if n == 0:
                 value = turned(value)
-            buf[g, pl.ds(BLOCK, SEL), :] = value.astype(BF16)
-            buf[g, pl.ds(BLOCK + SEL, FRESH - SEL), :] = jnp.zeros((FRESH - SEL, 128), BF16)
+            made_kv[0, n, pl.ds(0, SEL), pl.ds(g * 128, 128)] = value.astype(BF16)
             fresh[pl.ds(2 * n + g, SEL, stride=4), :] = value
         fresh_copies[n].start()
+    for copy in weights:
+        copy.start()
+
+    def put_in(n):
+        replaced = row_pos[pl.ds(blocks[n], 1), :]
+        source = jnp.concatenate(
+            [made_kv[n, 0], made_kv[n, 1], jnp.ones((FRESH, 128), BF16)], 1
+        )
+        for first in range(0, BLOCK, 256):
+            there = blocks[n] * BLOCK + first + lax.broadcasted_iota(jnp.int32, (256, 128), 0)
+            usable = lax.broadcasted_iota(jnp.int32, (256, 128), 1) < SEL
+            chosen = jnp.logical_and(there.astype(F32) == replaced, usable)
+            rows = jnp.dot(
+                jnp.where(chosen, 1.0, 0.0).astype(BF16), source, preferred_element_type=F32
+            )
+            gone = rows[:, 512:] > 0.5
+            where = pl.ds(n * BLOCK + first, 256)
+            for k, (buf, g) in enumerate(((kbuf, 0), (kbuf, 1), (vbuf, 0), (vbuf, 1))):
+                old = buf[g, where, :].astype(F32)
+                buf[g, where, :] = jnp.where(gone, rows[:, k * 128 : (k + 1) * 128], old).astype(
+                    BF16
+                )
+
+    for copy in stored_copies:
+        copy.wait_send()
+    put_in(0)
     new_ref[...] = fresh[...].astype(BF16)
 
     def full(g, da, db):
@@ -477,6 +503,7 @@
 
     for copy in stored_copies + fresh_copies:
         copy.wait_recv()
+    put_in(1)
     arrive(jnp.int32(0), 0)
     score(0, 0)
 
@@ -558,7 +585,7 @@
         copy.wait_recv()
     out_ref[...] = (total + zrecv[0].astype(F32) + zrecv[1].astype(F32)).astype(BF16)
 
-    for copy in stored_copies + fresh_copies:
+    for copy in fresh_copies:
         copy.wait_send()
     for g in range(2):
         for copy in a_sends(g) + [a_forward(g, 3), a_forward(g, 1)]:
@@ -602,6 +629,7 @@
             pltpu.VMEM((4 * BLOCK, 128), BF16),
             pltpu.VMEM((4 * BLOCK, 128), F32),
             pltpu.VMEM((4 * SEL, 128), F32),
+            pltpu.VMEM((2, 2, FRESH, 256), BF16),
             pltpu.VMEM((1, KEYS), F32),
             pltpu.VMEM((2, 16, ROWS, 128), BF16),
             pltpu.VMEM((2, KEYS, 128), BF16),

time: 78.6 us -> 77.2 us (0.982)
  Pallas kernels: 75.8 us -> 74.1 us
    pallas_call x1, Pallas kernels: 75.8 us -> 74.1 us  [attend(): pl.pallas_call(kernel, out_shape=(pltpu.VMEM((SEL, 1024), BF16), pltpu.VM...]
where the time goes in v4:
time: 77.2 us; the launch traced here: 76.6 us
  Pallas kernels  74.1 us (96%)
  local copies, waits for them, and re-layouts  1.32 us (2%)
    pallas_call x1, Pallas kernels, attend(): pl.pallas_call(kernel, out_shape=(pltpu.VMEM((SEL, 1024), BF16), pltpu.VM...  74.1 us

profile of v4, /device:TPU:0, one launch (start us, length us, event | category | flops | bytes accessed | tf_op | source)
XLA Modules:
  0.0 76.6 jit_solution(12063125319477130507)
XLA Ops:
  0.6 0.5 fusion.3.freq_in
  1.2 74.1 %shard_map.113 = (bf16[96,1024]{1,0:T(8,128)(2,1)S(1)}, bf16[384,128]{1,0:T(8,128)(2,1)S(1)}) custom-call(s32[8]{0:T(128)} %order_in.1, s32[8]{0:T(128)} %slot_in.1, bf16[96,4096]{1,0:T(8,128)(2,1)} %hidden_in.1, f32[1,4096]{1,0:T(1,128)} %bitcast.6, f32[1,128]{1,0:T(1,128)} %fusion.3.freq_in, s32[24,128]{1,0:T(8,128)} %bitcast.7, ...), custom_call_target="tpu_custom_call" | custom-call | tf_op jit(solution)/shard_map/pallas_call | solution.py:610
  75.3 0.7 copy.14
  75.9 0.6 copy.15

commit v5 on v4

--- a/solution.py
+++ b/solution.py
@@ -28,8 +28,8 @@
 
 
 WALK = (
-    (0, 1), (0, 3), (0, 2), (1, 1), (1, 3), (3, 1), (3, 3), (1, 2),
-    (3, 2), (2, 1), (2, 3), (2, 2), (1, 0), (2, 0), (3, 0), (0, 0),
+    (0, 1), (0, 3), (0, 2), (1, 1), (1, 3), (3, 1), (3, 3), (2, 1),
+    (2, 3), (1, 2), (2, 2), (3, 2), (2, 0), (1, 0), (3, 0), (0, 0),
 )
 OWN = {da: t for t, (da, db) in enumerate(WALK) if db == 0}
 
@@ -383,39 +383,41 @@
             halved(g, 0, da * 4 + db, half, 0, peer(g, 1, 0)).wait_recv()
 
     def arrive(t, g):
-        @pl.when(t == 0)
+        @pl.when(t < 3)
         def _():
+            @pl.when(t == 0)
+            def _():
+                for db in (1, 3):
+                    full(g, 0, db)
+                for copy in b_forwards(g, 0):
+                    copy.start()
+                for da in (1, 3):
+                    full(g, da, 0)
+                    a_forward(g, da).start()
+
+            @pl.when(t == 1)
+            def _():
+                for copy in b_sends(g, 1) + b_sends(g, 3):
+                    copy.start()
+
+            @pl.when(t == 2)
+            def _():
+                both_halves(g, 0, 2)
+                both_halves(g, 2, 0)
+                for copy in b_sends(g, 2):
+                    copy.start()
+
+        @pl.when(jnp.logical_or(jnp.logical_or(t == 3, t == 5), t == 7))
+        def _():
+            da = jnp.where(t == 3, 1, jnp.where(t == 5, 3, 2))
             for db in (1, 3):
-                full(g, 0, db)
-            for copy in b_forwards(g, 0):
+                full(g, da, db)
+            for copy in b_forwards(g, da):
                 copy.start()
-            for da in (1, 3):
-                full(g, da, 0)
-                a_forward(g, da).start()
-            for copy in b_sends(g, 1) + b_sends(g, 3):
-                copy.start()
-
-        @pl.when(t == 2)
+
+        @pl.when(jnp.logical_and(t >= 9, t < 12))
         def _():
-            both_halves(g, 0, 2)
-            both_halves(g, 2, 0)
-            for copy in b_sends(g, 2):
-                copy.start()
-
-        for first, da in ((3, 1), (5, 3), (9, 2)):
-
-            @pl.when(t == first)
-            def _(da=da):
-                for db in (1, 3):
-                    full(g, da, db)
-                for copy in b_forwards(g, da):
-                    copy.start()
-
-        for last, da in ((7, 1), (8, 3), (11, 2)):
-
-            @pl.when(t == last)
-            def _(da=da):
-                both_halves(g, da, 2)
+            both_halves(g, t - 8, 2)
 
     def score(t, g):
         da, db = offset(t, 0), offset(t, 1)
@@ -478,28 +480,32 @@
         ]
 
     def line(g, da):
-        for db in range(1, SIDE):
-            for copy in b_result(g, 0, da, db):
-                copy.wait_recv()
         t = OWN[da]
         return (
             [part[g, t]] + [rb_part[g, da, n] for n in range(3)],
             [stat[g, t]] + [rb_stat[g, da, n] for n in range(3)],
         )
 
-    def finish_line(da):
+    def line_arrives(da):
+        for g in range(2):
+            for db in range(1, SIDE):
+                for copy in b_result(g, 0, da, db):
+                    copy.wait_recv()
+
+    def merge_line(da):
         for g in range(2):
             merged, logs = merge(*line(g, da))
             mid[g, da - 1] = merged.astype(BF16)
             mid_stat[g, da - 1] = logs
+
+    def send_line(da):
+        for g in range(2):
             for copy in a_result(g, da):
                 copy.start()
 
     def pass_on(t, g):
-        @pl.when(t < 12)
-        def _():
-            for copy in b_result(g, t, offset(t, 0), offset(t, 1)):
-                copy.start()
+        for copy in b_result(g, t, offset(t, 0), offset(t, 1)):
+            copy.start()
 
     for copy in stored_copies + fresh_copies:
         copy.wait_recv()
@@ -509,12 +515,6 @@
 
     def step(t, carry):
         arrive(t, 1)
-        for da in (1, 2):
-
-            @pl.when(t == OWN[da] + 1)
-            def _(da=da):
-                finish_line(da)
-
         score(t, 1)
         weigh(t, 0)
         pass_on(t, 0)
@@ -524,11 +524,25 @@
         pass_on(t, 1)
         return carry
 
-    lax.fori_loop(0, 15, step, 0)
-    finish_line(3)
+    lax.fori_loop(0, 12, step, 0)
+    for t, da in ((12, None), (13, 2), (14, 1)):
+        if da is not None:
+            line_arrives(da)
+        score(t, 1)
+        weigh(t, 0)
+        if da is not None:
+            merge_line(da)
+        score(t + 1, 0)
+        weigh(t, 1)
+        if da is not None:
+            send_line(da)
+    line_arrives(3)
     score(15, 1)
     weigh(15, 0)
+    merge_line(3)
+    send_line(3)
     weigh(15, 1)
+    line_arrives(0)
     for g in range(2):
         parts, stats = line(g, 0)
         for da in (1, 2, 3):

time: 77.2 us -> 73.7 us (0.955)
  Pallas kernels: 74.1 us -> 71 us
    pallas_call x1, Pallas kernels: 74.1 us -> 71 us  [attend(): pl.pallas_call(kernel, out_shape=(pltpu.VMEM((SEL, 1024), BF16), pltpu.VM...]
where the time goes in v5:
time: 73.7 us; the launch traced here: 73.5 us
  Pallas kernels  71 us (96%)
  local copies, waits for them, and re-layouts  1.32 us (2%)
    pallas_call x1, Pallas kernels, attend(): pl.pallas_call(kernel, out_shape=(pltpu.VMEM((SEL, 1024), BF16), pltpu.VM...  71 us

profile of v5, /device:TPU:0, one launch (start us, length us, event | category | flops | bytes accessed | tf_op | source)
XLA Modules:
  0.0 73.5 jit_solution(15288560257823377556)
XLA Ops:
  0.6 0.5 fusion.3.freq_in
  1.2 71.0 %shard_map.113 = (bf16[96,1024]{1,0:T(8,128)(2,1)S(1)}, bf16[384,128]{1,0:T(8,128)(2,1)S(1)}) custom-call(s32[8]{0:T(128)} %order_in.1, s32[8]{0:T(128)} %slot_in.1, bf16[96,4096]{1,0:T(8,128)(2,1)} %hidden_in.1, f32[1,4096]{1,0:T(1,128)} %bitcast.6, f32[1,128]{1,0:T(1,128)} %fusion.3.freq_in, s32[24,128]{1,0:T(8,128)} %bitcast.7, ...), custom_call_target="tpu_custom_call" | custom-call | tf_op jit(solution)/shard_map/pallas_call | solution.py:624
  72.2 0.7 copy.14
  72.9 0.6 copy.15

commit v6 on v5

--- a/solution.py
+++ b/solution.py
@@ -28,8 +28,8 @@
 
 
 WALK = (
-    (0, 1), (0, 3), (0, 2), (1, 1), (1, 3), (3, 1), (3, 3), (2, 1),
-    (2, 3), (1, 2), (2, 2), (3, 2), (2, 0), (1, 0), (3, 0), (0, 0),
+    (0, 0), (0, 1), (0, 3), (0, 2), (1, 1), (1, 3), (3, 1), (3, 3),
+    (2, 1), (2, 3), (1, 2), (2, 2), (3, 2), (2, 0), (1, 0), (3, 0),
 )
 OWN = {da: t for t, (da, db) in enumerate(WALK) if db == 0}
 
@@ -383,9 +383,9 @@
             halved(g, 0, da * 4 + db, half, 0, peer(g, 1, 0)).wait_recv()
 
     def arrive(t, g):
-        @pl.when(t < 3)
+        @pl.when(t < 4)
         def _():
-            @pl.when(t == 0)
+            @pl.when(t == 1)
             def _():
                 for db in (1, 3):
                     full(g, 0, db)
@@ -395,29 +395,29 @@
                     full(g, da, 0)
                     a_forward(g, da).start()
 
-            @pl.when(t == 1)
+            @pl.when(t == 2)
             def _():
                 for copy in b_sends(g, 1) + b_sends(g, 3):
                     copy.start()
 
-            @pl.when(t == 2)
+            @pl.when(t == 3)
             def _():
                 both_halves(g, 0, 2)
                 both_halves(g, 2, 0)
                 for copy in b_sends(g, 2):
                     copy.start()
 
-        @pl.when(jnp.logical_or(jnp.logical_or(t == 3, t == 5), t == 7))
+        @pl.when(jnp.logical_or(jnp.logical_or(t == 4, t == 6), t == 8))
         def _():
-            da = jnp.where(t == 3, 1, jnp.where(t == 5, 3, 2))
+            da = jnp.where(t == 4, 1, jnp.where(t == 6, 3, 2))
             for db in (1, 3):
                 full(g, da, db)
             for copy in b_forwards(g, da):
                 copy.start()
 
-        @pl.when(jnp.logical_and(t >= 9, t < 12))
+        @pl.when(jnp.logical_and(t >= 10, t < 13))
         def _():
-            both_halves(g, t - 8, 2)
+            both_halves(g, t - 9, 2)
 
     def score(t, g):
         da, db = offset(t, 0), offset(t, 1)
@@ -492,14 +492,14 @@
                 for copy in b_result(g, 0, da, db):
                     copy.wait_recv()
 
-    def merge_line(da):
-        for g in range(2):
+    def merge_line(da, halves=(0, 1)):
+        for g in halves:
             merged, logs = merge(*line(g, da))
             mid[g, da - 1] = merged.astype(BF16)
             mid_stat[g, da - 1] = logs
 
-    def send_line(da):
-        for g in range(2):
+    def send_line(da, halves=(0, 1)):
+        for g in halves:
             for copy in a_result(g, da):
                 copy.start()
 
@@ -510,8 +510,12 @@
     for copy in stored_copies + fresh_copies:
         copy.wait_recv()
     put_in(1)
-    arrive(jnp.int32(0), 0)
     score(0, 0)
+    score(0, 1)
+    weigh(0, 0)
+    arrive(jnp.int32(1), 0)
+    score(1, 0)
+    weigh(0, 1)
 
     def step(t, carry):
         arrive(t, 1)
@@ -524,32 +528,43 @@
         pass_on(t, 1)
         return carry
 
-    lax.fori_loop(0, 12, step, 0)
-    for t, da in ((12, None), (13, 2), (14, 1)):
-        if da is not None:
-            line_arrives(da)
-        score(t, 1)
-        weigh(t, 0)
-        if da is not None:
-            merge_line(da)
-        score(t + 1, 0)
-        weigh(t, 1)
-        if da is not None:
-            send_line(da)
+    lax.fori_loop(1, 13, step, 0)
+    line_arrives(0)
+    score(13, 1)
+    weigh(13, 0)
+    for g in range(2):
+        merged, logs = merge(*line(g, 0))
+        part[g, 0] = merged.astype(BF16)
+        stat[g, 0] = logs
+    score(14, 0)
+    weigh(13, 1)
+    line_arrives(2)
+    score(14, 1)
+    weigh(14, 0)
+    merge_line(2)
+    send_line(2)
+    line_arrives(1)
+    score(15, 0)
+    weigh(14, 1)
+    merge_line(1, (0,))
+    send_line(1, (0,))
     line_arrives(3)
     score(15, 1)
     weigh(15, 0)
-    merge_line(3)
-    send_line(3)
+    merge_line(1, (1,))
+    send_line(1, (1,))
     weigh(15, 1)
-    line_arrives(0)
+    merge_line(3, (0,))
+    send_line(3, (0,))
+    merge_line(3, (1,))
+    send_line(3, (1,))
     for g in range(2):
-        parts, stats = line(g, 0)
-        for da in (1, 2, 3):
+        for da in (2, 1, 3):
             for copy in a_result(g, da):
                 copy.wait_recv()
         merged, _ = merge(
-            parts + [ra_part[g, n] for n in range(3)], stats + [ra_stat[g, n] for n in range(3)]
+            [part[g, 0]] + [ra_part[g, n] for n in range(3)],
+            [stat[g, 0]] + [ra_stat[g, n] for n in range(3)],
         )
         for h in range(GROUP):
             ctx[:, pl.ds((g * GROUP + h) * 128, 128)] = merged[h * SEL : (h + 1) * SEL].astype(BF16)

time: 73.7 us -> 74.2 us (level)
  no operation moved by 1% of the time
where the time goes in v6:
time: 74.2 us; the launch traced here: 73.9 us
  Pallas kernels  71.4 us (96%)
  local copies, waits for them, and re-layouts  1.32 us (2%)
    pallas_call x1, Pallas kernels, attend(): pl.pallas_call(kernel, out_shape=(pltpu.VMEM((SEL, 1024), BF16), pltpu.VM...  71.4 us

profile of v6, /device:TPU:0, one launch (start us, length us, event | category | flops | bytes accessed | tf_op | source)
XLA Modules:
  0.0 73.9 jit_solution(559685938463957114)
XLA Ops:
  0.6 0.5 fusion.3.freq_in
  1.2 71.4 %shard_map.113 = (bf16[96,1024]{1,0:T(8,128)(2,1)S(1)}, bf16[384,128]{1,0:T(8,128)(2,1)S(1)}) custom-call(s32[8]{0:T(128)} %order_in.1, s32[8]{0:T(128)} %slot_in.1, bf16[96,4096]{1,0:T(8,128)(2,1)} %hidden_in.1, f32[1,4096]{1,0:T(1,128)} %bitcast.6, f32[1,128]{1,0:T(1,128)} %fusion.3.freq_in, s32[24,128]{1,0:T(8,128)} %bitcast.7, ...), custom_call_target="tpu_custom_call" | custom-call | tf_op jit(solution)/shard_map/pallas_call | solution.py:639
  72.6 0.7 copy.14
  73.3 0.6 copy.15

commit v7 on v6

--- a/solution.py
+++ b/solution.py
@@ -242,7 +242,7 @@
 
     own_hidden.wait()
     own_stored.start()
-    q_loads[1][0].start()
+    kv_loads[0].start()
     widened = hid[...].astype(F32)
     mean = jnp.mean(widened * widened, -1, keepdims=True)
     normed[...] = (widened * lax.rsqrt(mean + 1e-05) * gain[...]).astype(BF16)
@@ -308,8 +308,9 @@
         return x * cos + pltpu.roll(x, HEAD_DIM // 2, 1) * sin
 
     pl.semaphore_wait(barrier, len(others))
-    later = {(0, 0): q_loads[1][1], (0, 1): kv_loads[0], (1, 0): kv_loads[1]}
-    for g in range(2):
+    later = {(0, 0): kv_loads[1], (0, 1): q_loads[1][0]}
+
+    def make_query(g):
         total = None
         for n in range(2):
             q_loads[g][n].wait()
@@ -327,14 +328,16 @@
             )
         for copy in a_sends(g) + b_sends(g, 0):
             copy.start()
-        if g == 0:
-            own_stored.wait()
-            wide[...] = stored[...].astype(F32)
-            for n, buf in enumerate((kbuf, vbuf)):
-                for k in range(2):
-                    rows = wide[pl.ds(2 * n + k, BLOCK, stride=4), :]
-                    buf[k, pl.ds(0, BLOCK), :] = rows.astype(BF16)
-                stored_copies[n].start()
+
+    make_query(0)
+    own_stored.wait()
+    q_loads[1][1].start()
+    wide[...] = stored[...].astype(F32)
+    for n, buf in enumerate((kbuf, vbuf)):
+        for g in range(2):
+            rows = wide[pl.ds(2 * n + g, BLOCK, stride=4), :]
+            buf[g, pl.ds(0, BLOCK), :] = rows.astype(BF16)
+        stored_copies[n].start()
 
     for n in range(2):
         kv_loads[n].wait()
@@ -347,6 +350,7 @@
             made_kv[0, n, pl.ds(0, SEL), pl.ds(g * 128, 128)] = value.astype(BF16)
             fresh[pl.ds(2 * n + g, SEL, stride=4), :] = value
         fresh_copies[n].start()
+    make_query(1)
     for copy in weights:
         copy.start()
 
@@ -394,10 +398,12 @@
                 for da in (1, 3):
                     full(g, da, 0)
                     a_forward(g, da).start()
+                for copy in b_sends(g, 1):
+                    copy.start()
 
             @pl.when(t == 2)
             def _():
-                for copy in b_sends(g, 1) + b_sends(g, 3):
+                for copy in b_sends(g, 3):
                     copy.start()
 
             @pl.when(t == 3)

time: 74.2 us -> 71.6 us (0.965)
  Pallas kernels: 71.4 us -> 69 us
    pallas_call x1, Pallas kernels: 71.4 us -> 69 us  [attend(): pl.pallas_call(kernel, out_shape=(pltpu.VMEM((SEL, 1024), BF16), pltpu.VM...]
where the time goes in v7:
time: 71.6 us; the launch traced here: 71.5 us
  Pallas kernels  69 us (96%)
  local copies, waits for them, and re-layouts  1.32 us (2%)
    pallas_call x1, Pallas kernels, attend(): pl.pallas_call(kernel, out_shape=(pltpu.VMEM((SEL, 1024), BF16), pltpu.VM...  69 us

profile of v7, /device:TPU:0, one launch (start us, length us, event | category | flops | bytes accessed | tf_op | source)
XLA Modules:
  0.0 71.5 jit_solution(15798018543175313447)
XLA Ops:
  0.6 0.5 fusion.3.freq_in
  1.2 69.0 %shard_map.113 = (bf16[96,1024]{1,0:T(8,128)(2,1)S(1)}, bf16[384,128]{1,0:T(8,128)(2,1)S(1)}) custom-call(s32[8]{0:T(128)} %order_in.1, s32[8]{0:T(128)} %slot_in.1, bf16[96,4096]{1,0:T(8,128)(2,1)} %hidden_in.1, f32[1,4096]{1,0:T(1,128)} %bitcast.6, f32[1,128]{1,0:T(1,128)} %fusion.3.freq_in, s32[24,128]{1,0:T(8,128)} %bitcast.7, ...), custom_call_target="tpu_custom_call" | custom-call | tf_op jit(solution)/shard_map/pallas_call | solution.py:645
  70.2 0.7 copy.14
  70.8 0.6 copy.15

commit v8 on v7

--- a/solution.py
+++ b/solution.py
@@ -398,12 +398,7 @@
                 for da in (1, 3):
                     full(g, da, 0)
                     a_forward(g, da).start()
-                for copy in b_sends(g, 1):
-                    copy.start()
-
-            @pl.when(t == 2)
-            def _():
-                for copy in b_sends(g, 3):
+                for copy in b_sends(g, 1) + b_sends(g, 3):
                     copy.start()
 
             @pl.when(t == 3)

time: 71.6 us -> 73.7 us (1.029)
  Pallas kernels: 69 us -> 71.1 us
    pallas_call x1, Pallas kernels: 69 us -> 71.1 us  [attend(): pl.pallas_call(kernel, out_shape=(pltpu.VMEM((SEL, 1024), BF16), pltpu.VM...]
where the time goes in v8:
time: 73.7 us; the launch traced here: 73.6 us
  Pallas kernels  71.1 us (96%)
  local copies, waits for them, and re-layouts  1.32 us (2%)
    pallas_call x1, Pallas kernels, attend(): pl.pallas_call(kernel, out_shape=(pltpu.VMEM((SEL, 1024), BF16), pltpu.VM...  71.1 us

profile of v8, /device:TPU:0, one launch (start us, length us, event | category | flops | bytes accessed | tf_op | source)
XLA Modules:
  0.0 73.6 jit_solution(8115251750078557509)
XLA Ops:
  0.6 0.5 fusion.3.freq_in
  1.2 71.1 %shard_map.113 = (bf16[96,1024]{1,0:T(8,128)(2,1)S(1)}, bf16[384,128]{1,0:T(8,128)(2,1)S(1)}) custom-call(s32[8]{0:T(128)} %order_in.1, s32[8]{0:T(128)} %slot_in.1, bf16[96,4096]{1,0:T(8,128)(2,1)} %hidden_in.1, f32[1,4096]{1,0:T(1,128)} %bitcast.6, f32[1,128]{1,0:T(1,128)} %fusion.3.freq_in, s32[24,128]{1,0:T(8,128)} %bitcast.7, ...), custom_call_target="tpu_custom_call" | custom-call | tf_op jit(solution)/shard_map/pallas_call | solution.py:640
  72.3 0.7 copy.14
  72.9 0.6 copy.15
